TPU v7x, 256 devices: a whole 4x4x8 slice. The times are simulated.
256 devices in a mesh: leaf: 64 (over z, x, core), sub: 4 (over y).
Axes of the slice: x: 4, y: 4, z: 8, core: 2. Of those that a mesh axis runs over, the one named last changes fastest.
Arguments:
- coords: bfloat16 [32768, 3, 128], P('leaf'), may hold values from 0 to 4
- charges: bfloat16 [32768, 8, 128], P(('leaf', 'sub')), may hold values from -6 to 6
- counts: int32 [32768], P('leaf'), may hold values from 32 to 128, as said below
- morton: int32 [32768], P('leaf'), may hold values from 0 to 511, as said below
- near_list: int32 [32768, 27], P(('leaf', 'sub')), may hold values from -1 to 32767, as said below
- basis: bfloat16 [32768, 64, 128], P(('leaf', 'sub')), may hold values from -0.5 to 0.5
- transfer1: bfloat16 [32768, 64, 64], P(('leaf', 'sub')), may hold values from -0.75 to 0.75
- far2_list: int32 [4096, 16], P(('leaf', 'sub')), may hold values from -1 to 4095, as said below
- coupling2: bfloat16 [4096, 16, 64, 64], P(('leaf', 'sub')), may hold values from -0.0625 to 0.0625
- transfer2: bfloat16 [4096, 64, 64], P('leaf'), may hold values from -0.75 to 0.75
- far3_list: int32 [64, 8], P('leaf'), may hold values from -1 to 63, as said below
- coupling3: bfloat16 [64, 8, 64, 64], P('leaf'), may hold values from -0.01171875 to 0.01171875
Outputs:
- potential: float32 [32768, 8, 128], P(('leaf', 'sub'))
Inputs may be any that keep to these rules, and one draw needn't show every extreme that they name: `counts`: each leaf's number of live points; leaves do not all have the same number. `morton`: within every block of 512 consecutive entries, a permutation of 0 to 511. `near_list`: row t starts with t itself; its other live entries are leaves other than t in the leaf group of t or in the group just before or after it; live entries come first and -1 fills the rest, with at least 13 live entries a row; entries may repeat. `far2_list`: row b names boxes other than b in the leaf group of b or in the group just before or after it; live entries come first and -1 fills the rest, with at least 8 live entries a row; entries may repeat. `far3_list`: row q names group boxes other than q; live entries come first and -1 fills the rest, with at least 4 live entries a row; entries may repeat.
All inputs are finite; a program needn't handle non-finite values.
Results may differ from a plain program's by a relative error of at most 0.011.
Values may be sent and summed in bfloat16 or wider, within the bound.
No kernel may reach another device: no remote copies, remote signals or barrier semaphores. Data moves between devices by JAX's collectives and lax.ppermute only.
A program may use at most 64 MiB of HBM per device.

v0:
```python
import functools

import jax
import jax.numpy as jnp
from jax import lax
from jax.experimental import pallas as pl
from jax.experimental.pallas import tpu as pltpu
from jax.sharding import PartitionSpec as P

kernel_scale = 0.07957747154594767
delta_squared = 0.0025

SLOTS = 4
UNITS = 16
STRIDE = 32
CLASSES = (128, 96, 64)
VMEM_LIMIT = 36 << 20


def shift(x, axis, by):
    count = lax.axis_size(axis)
    return lax.ppermute(x, axis, [(i, (i + by) % count) for i in range(count)])


def slide(x, axis, by):
    count = lax.axis_size(axis)
    pairs = [(i, i + by) for i in range(count) if 0 <= i + by < count]
    return lax.ppermute(x, axis, pairs)


def gather_ring(x, axis):
    count = lax.axis_size(axis)
    return [x] + [shift(x, axis, -k) for k in range(1, count)]


def prepare_targets(low, count, order, own_ref, tile_t):
    pick = lax.broadcasted_iota(jnp.int32, (8, 384), 1) // 128
    pick = (pick == lax.broadcasted_iota(jnp.int32, (8, 384), 0)).astype(jnp.bfloat16)
    targets = own_ref.shape[0]

    def body(w, _):
        for j in range(8):
            row = w * 8 + j
            own = own_ref[order[jnp.minimum(low + row, targets - 1)]]
            x = jnp.concatenate([own, jnp.zeros((4, 128), jnp.float32)], axis=0)
            wide = jnp.dot(x.T.astype(jnp.bfloat16), pick, preferred_element_type=jnp.float32)
            for c in range(3):
                tile_t[row * 3 + c] = wide[:, 128 * c : 128 * c + 128]
        return 0

    lax.fori_loop(0, (count + 7) // 8, body, 0)
    for c in range(3):
        tile_t[targets * 3 + c] = jnp.zeros((128, 128), jnp.float32)


def arrange_kernel(place, counts, b0, b1, b2, b3, out_ref, held, sems):
    rows = b0.shape[0]
    copies = [
        pltpu.make_async_copy(b, held.at[pl.ds(k * rows, rows)], sems.at[k])
        for k, b in enumerate((b0, b1, b2, b3))
    ]
    for copy in copies:
        copy.start()
    for copy in copies:
        copy.wait()
    point = lax.broadcasted_iota(jnp.int32, (8, 128), 1)

    def body(w, _):
        for j in range(16):
            s = w * 16 + j
            row = held[place[s]].astype(jnp.float32)
            out_ref[s] = jnp.where(point < counts[s], row, 0.0).astype(jnp.bfloat16)
        return 0

    lax.fori_loop(0, out_ref.shape[0] // 16, body, 0)


def arrange(place, counts, blocks):
    leaves = place.shape[0]
    whole = pl.BlockSpec(memory_space=pl.ANY)
    return pl.pallas_call(
        arrange_kernel,
        out_shape=jax.ShapeDtypeStruct((leaves, 8, 128), jnp.bfloat16),
        grid_spec=pltpu.PrefetchScalarGridSpec(
            num_scalar_prefetch=2,
            grid=(),
            in_specs=[whole] * 4,
            out_specs=pl.BlockSpec(memory_space=pltpu.VMEM),
            scratch_shapes=[
                pltpu.VMEM((leaves, 8, 128), jnp.bfloat16),
                pltpu.SemaphoreType.DMA((4,)),
            ],
        ),
        compiler_params=pltpu.CompilerParams(vmem_limit_bytes=8 << 20),
        cost_estimate=pl.CostEstimate(flops=1 << 20, bytes_accessed=2 << 20, transcendentals=0),
        name="arrange",
    )(place, counts, *blocks)


def near_steps(plan, low, high, own_ref, tile_t, src_c, src_q, acc, away):
    words, lists, bounds, ranks, order = plan
    bf = jnp.bfloat16
    targets = own_ref.shape[0]

    def rank_of(u):
        return ranks[lax.shift_right_logical(words[u], 5)]

    end = jnp.minimum(high * UNITS, bounds[4])
    some = end > low * UNITS
    base = jnp.where(some, rank_of(jnp.where(some, low * UNITS, 0)), 0)
    count = jnp.where(some, rank_of(jnp.where(some, end - 1, 0)) + 1 - base, 0)
    prepare_targets(base, count, order, own_ref, tile_t)

    def unit(word, rows):
        t = lax.shift_right_logical(word, 5)
        at = 3 * jnp.clip(ranks[t] - base, 0, targets)
        ids = [lists[word + k] - away for k in range(SLOTS)]
        charge = jnp.concatenate([src_q[i] for i in ids], axis=1)
        target = [
            [tile_t[at + c, 16 * m : 16 * m + 16, :].astype(bf) for c in range(3)]
            for m in range(rows // 16)
        ]
        columns = []
        for i in ids:
            source = [
                jnp.broadcast_to(src_c[i, c : c + 1, :], (16, 128)).astype(bf) for c in range(3)
            ]
            pieces = []
            for m in range(rows // 16):
                squared = None
                for c in range(3):
                    offset = target[m][c] - source[c]
                    if squared is None:
                        squared = offset * offset + jnp.asarray(delta_squared, bf)
                    else:
                        squared = squared + offset * offset
                pieces.append(lax.rsqrt(squared))
            columns.append(jnp.concatenate(pieces, axis=0))
        tile = jnp.concatenate(columns, axis=1)
        return t, lax.dot_general(
            charge, tile, (((1,), (1,)), ((), ())), preferred_element_type=jnp.float32
        )

    def step(rows, w, _):
        done = [unit(words[w * UNITS + j], rows) for j in range(UNITS)]
        for t, part in done:
            if rows < 128:
                part = jnp.concatenate([part, jnp.zeros((8, 128 - rows), jnp.float32)], axis=1)
            acc[t] = acc[t] + part * kernel_scale
        return 0

    for k, rows in enumerate(CLASSES):
        first = jnp.maximum(bounds[k], low)
        last = jnp.minimum(bounds[k + 1], high)
        lax.fori_loop(first, jnp.maximum(first, last), functools.partial(step, rows), 0)


def near_own_kernel(w, l, b, r, o, own_ref, c_ref, q_ref, acc, tile_t, src_c, src_q, sems):
    group = q_ref.shape[0]
    copies = [
        pltpu.make_async_copy(c_ref, src_c.at[pl.ds(0, group)], sems.at[0]),
        pltpu.make_async_copy(q_ref, src_q.at[pl.ds(0, group)], sems.at[1]),
    ]
    for copy in copies:
        copy.start()
    src_c[group] = jnp.zeros(src_c.shape[1:], src_c.dtype)
    src_q[group] = jnp.zeros(src_q.shape[1:], src_q.dtype)
    acc[...] = jnp.zeros_like(acc)
    for copy in copies:
        copy.wait()
    near_steps((w, l, b, r, o), 0, b[3], own_ref, tile_t, src_c, src_q, acc, group)


def near_first_kernel(
    share, w, l, b, r, o, own_ref, c0, c1, c2, q0, q1, q2, acc_in, acc, src_c, src_q, tile_t, sems
):
    group = q0.shape[0]
    copies = []
    for k, (c, q) in enumerate(((c0, q0), (c1, q1), (c2, q2))):
        rows = pl.ds(k * group, group)
        copies.append(pltpu.make_async_copy(c, src_c.at[rows], sems.at[k, 0]))
        copies.append(pltpu.make_async_copy(q, src_q.at[rows], sems.at[k, 1]))
    for copy in copies:
        copy.start()
    src_c[3 * group] = jnp.zeros(src_c.shape[1:], src_c.dtype)
    src_q[3 * group] = jnp.zeros(src_q.shape[1:], src_q.dtype)
    acc[...] = acc_in[...]
    for copy in copies:
        copy.wait()
    high = b[3] * share[1] // share[2]
    near_steps((w, l, b, r, o), 0, high, own_ref, tile_t, src_c, src_q, acc, 0)


def near_next_kernel(share, w, l, b, r, o, own_ref, src_c, src_q, acc_in, acc, tile_t):
    acc[...] = acc_in[...]
    low = b[3] * share[0] // share[2]
    high = b[3] * share[1] // share[2]
    near_steps((w, l, b, r, o), low, high, own_ref, tile_t, src_c, src_q, acc, 0)


near_params = pltpu.CompilerParams(vmem_limit_bytes=VMEM_LIMIT)
near_cost = pl.CostEstimate(flops=1 << 32, bytes_accessed=1 << 20, transcendentals=50 << 20)
in_vmem = pl.BlockSpec(memory_space=pltpu.VMEM)
in_place = pl.BlockSpec(memory_space=pl.ANY)


def tile_scratch(targets):
    return pltpu.VMEM((targets * 3 + 3, 128, 128), jnp.float32)


def near_own(plan, own_coords, coords, charges):
    group = charges.shape[0]
    targets = own_coords.shape[0]
    return pl.pallas_call(
        near_own_kernel,
        out_shape=jax.ShapeDtypeStruct((targets + 1, 8, 128), jnp.float32),
        grid_spec=pltpu.PrefetchScalarGridSpec(
            num_scalar_prefetch=5,
            grid=(),
            in_specs=[in_vmem] + [in_place] * 2,
            out_specs=in_vmem,
            scratch_shapes=[
                tile_scratch(targets),
                pltpu.VMEM((group + 1, 4, 128), jnp.float32),
                pltpu.VMEM((group + 1, 8, 128), jnp.bfloat16),
                pltpu.SemaphoreType.DMA((2,)),
            ],
        ),
        compiler_params=near_params,
        cost_estimate=near_cost,
        name="near_own",
    )(*plan, own_coords, coords, charges)


def near_first(share, plan, own_coords, coords, charges, acc):
    group = charges[0].shape[0]
    return pl.pallas_call(
        near_first_kernel,
        out_shape=(
            jax.ShapeDtypeStruct(acc.shape, jnp.float32),
            pltpu.VMEM((3 * group + 1, 4, 128), jnp.float32),
            pltpu.VMEM((3 * group + 1, 8, 128), jnp.bfloat16),
        ),
        grid_spec=pltpu.PrefetchScalarGridSpec(
            num_scalar_prefetch=6,
            grid=(),
            in_specs=[in_vmem] + [in_place] * 6 + [in_vmem],
            out_specs=(in_vmem,) * 3,
            scratch_shapes=[
                tile_scratch(own_coords.shape[0]),
                pltpu.SemaphoreType.DMA((3, 2)),
            ],
        ),
        compiler_params=near_params,
        cost_estimate=near_cost,
        name="near_first",
    )(share, *plan, own_coords, *coords, *charges, acc)


def near_next(share, plan, own_coords, src_c, src_q, acc):
    return pl.pallas_call(
        near_next_kernel,
        out_shape=jax.ShapeDtypeStruct(acc.shape, jnp.float32),
        grid_spec=pltpu.PrefetchScalarGridSpec(
            num_scalar_prefetch=6,
            grid=(),
            in_specs=[in_vmem] * 4,
            out_specs=in_vmem,
            scratch_shapes=[tile_scratch(own_coords.shape[0])],
        ),
        compiler_params=near_params,
        cost_estimate=near_cost,
        name="near_next",
    )(share, *plan, own_coords, src_c, src_q, acc)


def order_units(first, number, kind, targets, most):
    ids = jnp.arange(targets, dtype=jnp.int32)
    before = (kind[None, :] < kind[:, None]) | (
        (kind[None, :] == kind[:, None]) & (ids[None, :] < ids[:, None])
    )
    start = jnp.sum(jnp.where(before, number[None, :], 0), axis=1)
    classes = jnp.arange(len(CLASSES), dtype=jnp.int32)
    upto = jnp.sum(jnp.where(kind[None, :] <= classes[:, None], number[None, :], 0), axis=1)
    bounds = jnp.concatenate([jnp.zeros((1,), jnp.int32), (upto + UNITS - 1) // UNITS, upto[-1:]])
    unit = jnp.arange(most, dtype=jnp.int32)
    at = unit[:, None] - start[None, :]
    mine = (at >= 0) & (at < number[None, :])
    words = ids[None, :] * STRIDE + (first[None, :] + at) * SLOTS - targets * STRIDE
    return jnp.sum(jnp.where(mine, words, 0), axis=1) + targets * STRIDE, bounds


def plan_near(near_list, base, group, counts):
    targets, slots = near_list.shape
    dummy = 3 * group
    live = near_list >= 0
    local = jnp.where(live, jnp.clip(near_list - base, 0, dummy - 1), dummy)
    own = live & (local >= group) & (local < 2 * group)
    rest = live & ~own
    earlier = jnp.arange(slots)[:, None] < jnp.arange(slots)[None, :]
    own_number = jnp.sum(own, axis=1, dtype=jnp.int32)
    number = jnp.sum(live, axis=1, dtype=jnp.int32)
    own_rank = jnp.sum(own[:, :, None] & earlier[None], axis=1, dtype=jnp.int32)
    rest_rank = jnp.sum(rest[:, :, None] & earlier[None], axis=1, dtype=jnp.int32)
    rank = jnp.where(own, own_rank, jnp.where(rest, own_number[:, None] + rest_rank, STRIDE))
    slot = jnp.arange(STRIDE, dtype=jnp.int32)
    hit = rank[:, None, :] == slot[None, :, None]
    lists = jnp.sum(jnp.where(hit, local[:, None, :] - dummy, 0), axis=2) + dummy
    lists = jnp.pad(lists, ((0, 1), (0, 0)), constant_values=dummy).reshape(-1)
    kind = sum((counts <= rows).astype(jnp.int32) for rows in CLASSES[1:])
    whole = own_number // SLOTS
    units = (number + SLOTS - 1) // SLOTS
    most = targets * ((slots + SLOTS - 1) // SLOTS) + UNITS
    zero = jnp.zeros_like(whole)
    words_own, bounds_own = order_units(zero, whole, kind, targets, most)
    words_all, bounds_all = order_units(whole, units - whole, kind, targets, most)
    lists_own = jnp.where(lists == dummy, 2 * group, lists)
    ids = jnp.arange(targets, dtype=jnp.int32)
    before = (kind[None, :] < kind[:, None]) | (
        (kind[None, :] == kind[:, None]) & (ids[None, :] < ids[:, None])
    )
    ranks = jnp.sum(before, axis=1, dtype=jnp.int32)
    order = jnp.sum(jnp.where(ranks[None, :] == ids[:, None], ids[None, :], 0), axis=1)
    ranks = jnp.pad(ranks, (0, 1), constant_values=4 * targets)
    return (words_own, lists_own, bounds_own, ranks, order), (
        words_all,
        lists,
        bounds_all,
        ranks,
        order,
    )


def far_field(moments, lists, couplings, offset):
    valid = lists >= 0
    local = jnp.clip(lists - offset, 0, moments.shape[0] - 1)
    source = jnp.where(valid[..., None, None], moments[local], jnp.zeros((), moments.dtype))
    return jnp.einsum("bkrc,bkcp->brp", source, couplings, preferred_element_type=jnp.float32)


def on_device(
    coords,
    charges,
    counts,
    morton,
    near_list,
    basis,
    transfer1,
    far2_list,
    coupling2,
    transfer2,
    far3_list,
    coupling3,
):
    lane = lax.axis_index("sub")
    group = lax.axis_index("leaf")
    leaves = lax.axis_size("leaf")
    lanes = lax.axis_size("sub")
    leaf_dev, rhs_count, points = charges.shape
    rank_size = basis.shape[1]
    group_size = coords.shape[0]
    clusters = far2_list.shape[0]
    group_boxes = transfer2.shape[0]
    start = lane * leaf_dev

    tie = lax.optimization_barrier

    blocks = gather_ring(charges, "sub")
    own_counts = lax.dynamic_slice_in_dim(counts, start, leaf_dev, 0)
    wide = jnp.pad(coords.astype(jnp.float32), ((0, 0), (0, 1), (0, 0)))
    left_c = slide(wide, "leaf", 1)
    right_c = slide(wide, "leaf", -1)
    own_coords = lax.dynamic_slice_in_dim(wide, start, leaf_dev, 0)

    slot = jnp.arange(group_size, dtype=jnp.int32)
    inverse = jnp.sum(jnp.where(morton[None, :] == slot[:, None], slot[None, :], 0), axis=1)
    place = lax.rem(inverse // leaf_dev - lane + lanes, lanes) * leaf_dev + inverse % leaf_dev
    plan_own, plan_all = plan_near(near_list, (group - 1) * group_size, group_size, own_counts)

    blocks, left_c, right_c, plan_own, plan_all = tie((blocks, left_c, right_c, plan_own, plan_all))
    mine = arrange(place, counts, blocks)
    left_q = slide(mine, "leaf", 1)
    right_q = slide(mine, "leaf", -1)

    own_charges = lax.dynamic_slice_in_dim(mine, start, leaf_dev, 0)
    transfer_boxed = transfer1.reshape(clusters, 8, rank_size, rank_size)
    leaf_moments = jnp.einsum(
        "trp,tkp->trk", own_charges, basis, preferred_element_type=jnp.float32
    ).astype(jnp.bfloat16)
    box_moments = jnp.einsum(
        "bnrc,bncp->brp",
        leaf_moments.reshape(clusters, 8, rhs_count, rank_size),
        transfer_boxed,
        preferred_element_type=jnp.float32,
    ).astype(jnp.bfloat16)

    mine_after, box_moments = tie((mine, box_moments))
    ring = gather_ring(box_moments, "sub")
    acc = near_own(plan_own, own_coords, wide, mine_after)
    ring, acc = tie((ring, acc))
    group_moments = jnp.roll(jnp.stack(ring), lane, axis=0)
    group_moments = group_moments.reshape(group_boxes, rhs_count, rank_size)
    top_moment = jnp.einsum(
        "brc,bcp->rp", group_moments, transfer2, preferred_element_type=jnp.float32
    ).astype(jnp.bfloat16)

    table = top_moment[None]
    reach, rounds = 1, (leaves - 1).bit_length()
    for k in range(rounds):
        share = jnp.asarray([k, k + 1, rounds], jnp.int32)
        table, acc, group_moments = tie((table, acc, group_moments))
        other = lax.ppermute(table, "leaf", [(i, i ^ reach) for i in range(leaves)])
        if k == 0:
            acc, src_c, src_q = near_first(
                share, plan_all, own_coords, (left_c, wide, right_c), (left_q, mine, right_q), acc
            )
        else:
            acc = near_next(share, plan_all, own_coords, src_c, src_q, acc)
        if k == 1:
            left_b = slide(group_moments, "leaf", 1)
            right_b = slide(group_moments, "leaf", -1)
        if k == 3:
            table, left_b, right_b = tie((table, left_b, right_b))
        table = jnp.concatenate([table, other], axis=0)
        reach *= 2
    flipped = jnp.where(far3_list >= 0, far3_list ^ group, -1)
    top_field = far_field(table, flipped, coupling3, 0).astype(jnp.bfloat16)

    near_boxes = jnp.concatenate([left_b, group_moments, right_b], axis=0)
    box_far = far_field(near_boxes, far2_list, coupling2, (group - 1) * group_boxes)
    own_transfer = lax.dynamic_slice_in_dim(transfer2, lane * clusters, clusters, 0)
    box_local = (
        box_far
        + jnp.einsum("rp,bcp->brc", top_field[0], own_transfer, preferred_element_type=jnp.float32)
    ).astype(jnp.bfloat16)
    leaf_local = jnp.einsum(
        "brp,bncp->bnrc", box_local, transfer_boxed, preferred_element_type=jnp.float32
    ).astype(jnp.bfloat16)
    leaf_local = leaf_local.reshape(leaf_dev, rhs_count, rank_size)
    far_part = jnp.einsum("trk,tkp->trp", leaf_local, basis, preferred_element_type=jnp.float32)
    point = jnp.arange(points, dtype=jnp.int32)
    own_live = point[None, :] < own_counts[:, None]
    return jnp.where(own_live[:, None, :], acc[:leaf_dev] + far_part, jnp.zeros((), jnp.float32))


def solution(mesh):
    return jax.shard_map(
        on_device,
        mesh=mesh,
        in_specs=(
            P("leaf", None, None),
            P(("leaf", "sub"), None, None),
            P("leaf"),
            P("leaf"),
            P(("leaf", "sub"), None),
            P(("leaf", "sub"), None, None),
            P(("leaf", "sub"), None, None),
            P(("leaf", "sub"), None),
            P(("leaf", "sub"), None, None, None),
            P("leaf", None, None),
            P("leaf", None),
            P("leaf", None, None, None),
        ),
        out_specs=P(("leaf", "sub"), None, None),
        check_vma=False,
    )
```

profile of v0, /device:TPU:22, one launch (start us, length us, event | category | flops | bytes accessed | tf_op | source)
XLA Modules:
  0.0 141.8 jit_solution(6251904463641682774)
XLA Ops:
  0.6 2.9 %collective-permute-start.1 = (bf16[128,8,128]{2,1,0:T(8,128)(2,1)}, bf16[128,8,128]{2,1,0:T(8,128)(2,1)}, u32[]{:S(2)}, u32[]{:S(2)}) collective-permute-start(bf16[128,8,128]{2,1,0:T(8,128)(2,1)} %b0), channel_id=1, source_target_pairs={{0,2},{1,3},{2,0},{3,1},{4,6},{5,7},{6,4},{7,5},{8,10},{9,11},{10,... | collective-permute-start | bytes 786440 | tf_op jit(solution)/shard_map/ppermute | solution.py:22
  5.0 1.9 %collective-permute-start.3 = (f32[512,4,128]{2,1,0:T(4,128)S(1)}, f32[512,4,128]{2,1,0:T(4,128)}, u32[]{:S(2)}, u32[]{:S(2)}) collective-permute-start(f32[512,4,128]{2,1,0:T(4,128)S(1)} %pad_convert_fusion.c_ref.c1), channel_id=1, source_target_pairs={{0,4},{4,8},{8,12},{12,16},{16,20},{20,24},{24,28},{28,32},{32,36}... | collective-permute-start | bytes 3145736 | tf_op jit(solution)/shard_map/ppermute | solution.py:28
  7.0 3.6 %collective-permute-start.4 = (f32[512,4,128]{2,1,0:T(4,128)S(1)}, f32[512,4,128]{2,1,0:T(4,128)}, u32[]{:S(2)}, u32[]{:S(2)}) collective-permute-start(f32[512,4,128]{2,1,0:T(4,128)S(1)} %pad_convert_fusion.c_ref.c1), channel_id=1, source_target_pairs={{4,0},{8,4},{12,8},{16,12},{20,16},{24,20},{28,24},{32,28},{36,32}... | collective-permute-start | bytes 3145736 | tf_op jit(solution)/shard_map/ppermute | solution.py:28
  19.1 4.7 %copy.34 = bf16[128,64,64]{2,1,0:T(8,128)(2,1)} copy(bf16[128,64,64]{0,2,1:T(8,128)(2,1)} %param.24) | data formatting | bytes 2097152 | tf_op args[6]
  24.8 3.6 %arrange.1.q_ref.q1 = bf16[512,8,128]{2,1,0:T(8,128)(2,1)} custom-call(s32[512]{0:T(512)S(1)} %fusion.31.place, s32[512]{0:T(512)S(1)} %copy-done.2, bf16[128,8,128]{2,1,0:T(8,128)(2,1)S(1)} %copy-done.1, bf16[128,8,128]{2,1,0:T(8,128)(2,1)} %collective-permute-done.b1, bf16[128,8,128]{2,1,0:T(8,128)(2,1)} %collective-permute-done.1.b2, ...), custom_call_target="tpu_custom_call" | custom-call | flops 1048576 | bytes 2097152 | tf_op jit(solution)/shard_map/arrange/pallas_call | solution.py:81
  28.5 5.3 %collective-permute-start.5 = (bf16[512,8,128]{2,1,0:T(8,128)(2,1)}, bf16[512,8,128]{2,1,0:T(8,128)(2,1)}, u32[]{:S(2)}, u32[]{:S(2)}) collective-permute-start(bf16[512,8,128]{2,1,0:T(8,128)(2,1)} %arrange.1.q_ref.q1), channel_id=1, source_target_pairs={{0,4},{4,8},{8,12},{12,16},{16,20},{20,24},{24,28},{28,32},{32,36}... | collective-permute-start | bytes 3145736 | tf_op jit(solution)/shard_map/ppermute | solution.py:28
  33.8 1.9 %collective-permute-start.6 = (bf16[512,8,128]{2,1,0:T(8,128)(2,1)}, bf16[512,8,128]{2,1,0:T(8,128)(2,1)}, u32[]{:S(2)}, u32[]{:S(2)}) collective-permute-start(bf16[512,8,128]{2,1,0:T(8,128)(2,1)} %arrange.1.q_ref.q1), channel_id=1, source_target_pairs={{4,0},{8,4},{12,8},{16,12},{20,16},{24,20},{28,24},{32,28},{36,32}... | collective-permute-start | bytes 3145736 | tf_op jit(solution)/shard_map/ppermute | solution.py:28
  35.7 2.2 %convolution_convert_fusion.1 = bf16[128,8,64]{2,1,0:T(8,128)(2,1)S(1)} fusion(bf16[128,64,128]{2,1,0:T(8,128)(2,1)S(1)} %copy-done, bf16[512,8,128]{2,1,0:T(8,128)(2,1)} %arrange.1.q_ref.q1, s32[]{:T(128)S(6)} %select_n.131), kind=kOutput, calls=%fused_computation.3 | convolution fusion | flops 16842752 | bytes 2490372 | tf_op jit(solution)/shard_map/trp,tkp->trk/dot_general | solution.py:387
  38.3 2.1 %collective-permute-start.7 = (bf16[16,8,64]{2,1,0:T(8,128)(2,1)S(1)}, bf16[16,8,64]{2,1,0:T(8,128)(2,1)S(1)}, u32[]{:S(2)}, u32[]{:S(2)}) collective-permute-start(bf16[16,8,64]{2,1,0:T(8,128)(2,1)S(1)} %fusion.2), channel_id=1, source_target_pairs={{0,3},{1,0},{2,1},{3,2},{4,7},{5,4},{6,5},{7,6},{8,11},{9,8},{10,9... | collective-permute-start | bytes 49160 | tf_op jit(solution)/shard_map/ppermute | solution.py:22
  40.4 1.9 %collective-permute-start.8 = (bf16[16,8,64]{2,1,0:T(8,128)(2,1)S(1)}, bf16[16,8,64]{2,1,0:T(8,128)(2,1)S(1)}, u32[]{:S(2)}, u32[]{:S(2)}) collective-permute-start(bf16[16,8,64]{2,1,0:T(8,128)(2,1)S(1)} %fusion.2), channel_id=1, source_target_pairs={{0,2},{1,3},{2,0},{3,1},{4,6},{5,7},{6,4},{7,5},{8,10},{9,11},{10,... | collective-permute-start | bytes 49160 | tf_op jit(solution)/shard_map/ppermute | solution.py:22
  42.6 18.8 %near_own.1.acc_in = f32[129,8,128]{2,1,0:T(8,128)S(1)} custom-call(s32[912]{0:T(1024)S(1)} %get-tuple-element.64.w, s32[4128]{0:T(1024)S(1)} %compare_select_fusion.l, s32[5]{0:T(128)S(1)} %fusion.37.b, s32[129]{0:T(256)S(1)} %pad.17.r, s32[128]{0:T(128)S(1)} %select_reduce_fusion.5.o, f32[128,4,128]{2,1,0:T(4,128)S(1)} %constant_dynamic-slice_fusion.1.own_ref, ...), custom_call_target="tpu_custom_call" | custom-call | flops 4294967296 | bytes 1048576 | tf_op jit(solution)/shard_map/near_own/pallas_call | solution.py:214
  65.3 9.4 %near_first.1 = (f32[129,8,128]{2,1,0:T(8,128)S(1)}, f32[1537,4,128]{2,1,0:T(4,128)S(1)}, bf16[1537,8,128]{2,1,0:T(8,128)(2,1)S(1)}) custom-call(s32[3]{0:T(128)S(1)} %copy-done.8, s32[912]{0:T(1024)S(1)} %get-tuple-element.52.w, s32[4128]{0:T(1024)S(1)} %reshape.113.l, s32[5]{0:T(128)S(1)} %fusion.38.b, s32[129]{0:T(256)S(1)} %pad.17.r, ...), custom_call_target="tpu_custom_call" | custom-call | flops 4294967296 | bytes 1048576 | tf_op jit(solution)/shard_map/near_first/pallas_call | solution.py:237
  74.7 2.1 %collective-permute-start.13 = (bf16[64,8,64]{2,1,0:T(8,128)(2,1)S(1)}, bf16[64,8,64]{2,1,0:T(8,128)(2,1)S(1)}, u32[]{:S(2)}, u32[]{:S(2)}) collective-permute-start(bf16[64,8,64]{2,1,0:T(8,128)(2,1)S(1)} %bitcast.79), channel_id=1, source_target_pairs={{0,4},{4,8},{8,12},{12,16},{16,20},{20,24},{24,28},{28,32},{32,36}... | collective-permute-start | bytes 196616 | tf_op jit(solution)/shard_map/ppermute | solution.py:28
  76.8 3.5 %collective-permute-start.14 = (bf16[64,8,64]{2,1,0:T(8,128)(2,1)S(1)}, bf16[64,8,64]{2,1,0:T(8,128)(2,1)S(1)}, u32[]{:S(2)}, u32[]{:S(2)}) collective-permute-start(bf16[64,8,64]{2,1,0:T(8,128)(2,1)S(1)} %bitcast.80), channel_id=1, source_target_pairs={{4,0},{8,4},{12,8},{16,12},{20,16},{24,20},{28,24},{32,28},{36,32}... | collective-permute-start | bytes 196616 | tf_op jit(solution)/shard_map/ppermute | solution.py:28
  80.4 6.9 %near_next.5.acc_in = f32[129,8,128]{2,1,0:T(8,128)S(1)} custom-call(s32[3]{0:T(128)S(1)} %copy-done.7, s32[912]{0:T(1024)S(1)} %get-tuple-element.52.w, s32[4128]{0:T(1024)S(1)} %reshape.113.l, s32[5]{0:T(128)S(1)} %fusion.38.b, s32[129]{0:T(256)S(1)} %pad.17.r, s32[128]{0:T(128)S(1)} %select_reduce_fusion.5.o, ...), custom_call_target="tpu_custom_call" | custom-call | flops 4294967296 | bytes 1048576 | tf_op jit(solution)/shard_map/near_next/pallas_call | solution.py:261
  88.8 7.5 %near_next.6.acc_in = f32[129,8,128]{2,1,0:T(8,128)S(1)} custom-call(s32[3]{0:T(128)S(1)} %copy-done.6, s32[912]{0:T(1024)S(1)} %get-tuple-element.52.w, s32[4128]{0:T(1024)S(1)} %reshape.113.l, s32[5]{0:T(128)S(1)} %fusion.38.b, s32[129]{0:T(256)S(1)} %pad.17.r, s32[128]{0:T(128)S(1)} %select_reduce_fusion.5.o, ...), custom_call_target="tpu_custom_call" | custom-call | flops 4294967296 | bytes 1048576 | tf_op jit(solution)/shard_map/near_next/pallas_call | solution.py:261
  96.4 5.3 %collective-permute-start.15 = (bf16[8,8,64]{2,1,0:T(8,128)(2,1)S(1)}, bf16[8,8,64]{2,1,0:T(8,128)(2,1)S(1)}, u32[]{:S(2)}, u32[]{:S(2)}) collective-permute-start(bf16[8,8,64]{2,1,0:T(8,128)(2,1)S(1)} %pad_maximum_fusion.4), channel_id=1, source_target_pairs={{0,32},{4,36},{8,40},{12,44},{16,48},{20,52},{24,56},{28,60},{32,0... | collective-permute-start | bytes 24584 | tf_op jit(solution)/shard_map/ppermute | solution.py:412
  101.7 6.0 %near_next.7.acc_in = f32[129,8,128]{2,1,0:T(8,128)S(1)} custom-call(s32[3]{0:T(128)S(1)} %copy-done.5, s32[912]{0:T(1024)S(1)} %get-tuple-element.52.w, s32[4128]{0:T(1024)S(1)} %reshape.113.l, s32[5]{0:T(128)S(1)} %fusion.38.b, s32[129]{0:T(256)S(1)} %pad.17.r, s32[128]{0:T(128)S(1)} %select_reduce_fusion.5.o, ...), custom_call_target="tpu_custom_call" | custom-call | flops 4294967296 | bytes 1048576 | tf_op jit(solution)/shard_map/near_next/pallas_call | solution.py:261
  107.7 4.2 %collective-permute-start.16 = (bf16[16,8,64]{2,1,0:T(8,128)(2,1)S(1)}, bf16[16,8,64]{2,1,0:T(8,128)(2,1)S(1)}, u32[]{:S(2)}, u32[]{:S(2)}) collective-permute-start(bf16[16,8,64]{2,1,0:T(8,128)(2,1)S(1)} %pad_maximum_fusion.3), channel_id=1, source_target_pairs={{0,64},{4,68},{8,72},{12,76},{16,80},{20,84},{24,88},{28,92},{32,9... | collective-permute-start | bytes 49160 | tf_op jit(solution)/shard_map/ppermute | solution.py:412
  111.9 5.6 %near_next.8.acc_in = f32[129,8,128]{2,1,0:T(8,128)S(1)} custom-call(s32[3]{0:T(128)S(1)} %copy-done.4, s32[912]{0:T(1024)S(1)} %get-tuple-element.52.w, s32[4128]{0:T(1024)S(1)} %reshape.113.l, s32[5]{0:T(128)S(1)} %fusion.38.b, s32[129]{0:T(256)S(1)} %pad.17.r, s32[128]{0:T(128)S(1)} %select_reduce_fusion.5.o, ...), custom_call_target="tpu_custom_call" | custom-call | flops 4294967296 | bytes 1048576 | tf_op jit(solution)/shard_map/near_next/pallas_call | solution.py:261
  117.6 7.2 %collective-permute-start.17 = (bf16[32,8,64]{2,1,0:T(8,128)(2,1)S(1)}, bf16[32,8,64]{2,1,0:T(8,128)(2,1)S(1)}, u32[]{:S(2)}, u32[]{:S(2)}) collective-permute-start(bf16[32,8,64]{2,1,0:T(8,128)(2,1)S(1)} %pad_maximum_fusion.2), channel_id=1, source_target_pairs={{0,128},{4,132},{8,136},{12,140},{16,144},{20,148},{24,152},{28,15... | collective-permute-start | bytes 98312 | tf_op jit(solution)/shard_map/ppermute | solution.py:412
  124.8 5.6 %near_next.9 = f32[129,8,128]{2,1,0:T(8,128)S(1)} custom-call(s32[3]{0:T(128)S(1)} %copy-done.3, s32[912]{0:T(1024)S(1)} %get-tuple-element.52.w, s32[4128]{0:T(1024)S(1)} %reshape.113.l, s32[5]{0:T(128)S(1)} %fusion.38.b, s32[129]{0:T(256)S(1)} %pad.17.r, s32[128]{0:T(128)S(1)} %select_reduce_fusion.5.o, ...), custom_call_target="tpu_custom_call" | custom-call | flops 4294967296 | bytes 1048576 | tf_op jit(solution)/shard_map/near_next/pallas_call | solution.py:261
  132.1 3.6 %convolution_bitcast_fusion.1 = f32[16,8,64]{2,1,0:T(8,128)S(1)} fusion(bf16[16,16,64,64]{3,2,1,0:T(8,128)(2,1)} %param.26, bf16[16,16,8,64]{3,2,1,0:T(8,128)(2,1)} %bitcast.84, pred[16,16]{1,0:T(8,128)(4,1)S(1)} %copy-done.19), kind=kOutput, calls=%fused_computation.6 | convolution fusion | flops 16908288 | bytes 2392320 | tf_op jit(solution)/shard_map/bkrc,bkcp->brp/dot_general | solution.py:338
  136.7 3.6 %convolution_convert_fusion = bf16[16,8,8,64]{3,1,2,0:T(8,128)(2,1)S(1)} fusion(bf16[16,8,64,64]{3,2,1,0:T(8,128)(2,1)} %bitcast.76, f32[16,8,64]{2,1,0:T(8,128)S(1)} %convolution_bitcast_fusion.1, bf16[8,64,1]{1,0,2:T(8,128)(2,1)S(1)} %fusion.6, bf16[64,64,64]{2,1,0:T(8,128)(2,1)} %param.27, s32[]{:T(128)S(6)} %select_n.155), kind=kOutput, calls=%fused_computation.2 | convolution fusion | flops 9519104 | bytes 2524164 | tf_op jit(solution)/shard_map/brp,bncp->bnrc/dot_general | solution.py:436
  (133 shorter events, 21.8 us)
Async XLA Ops:
  0.0 35.7 %copy-start = (bf16[128,64,128]{2,1,0:T(8,128)(2,1)S(1)}, bf16[128,64,128]{2,1,0:T(8,128)(2,1)}, u32[]{:S(2)}) copy-start(bf16[128,64,128]{2,1,0:T(8,128)(2,1)} %param.23) | copy-start | bytes 6291460
  0.0 23.8 %collective-permute-start = (bf16[128,8,128]{2,1,0:T(8,128)(2,1)}, bf16[128,8,128]{2,1,0:T(8,128)(2,1)}, u32[]{:S(2)}, u32[]{:S(2)}) collective-permute-start(bf16[128,8,128]{2,1,0:T(8,128)(2,1)} %b0), channel_id=1, source_target_pairs={{0,3},{1,0},{2,1},{3,2},{4,7},{5,4},{6,5},{7,6},{8,11},{9,8},{10,9... | collective-permute-start | bytes 786440 | tf_op jit(solution)/shard_map/ppermute | solution.py:22
  0.6 23.3 %collective-permute-start.1 = (bf16[128,8,128]{2,1,0:T(8,128)(2,1)}, bf16[128,8,128]{2,1,0:T(8,128)(2,1)}, u32[]{:S(2)}, u32[]{:S(2)}) collective-permute-start(bf16[128,8,128]{2,1,0:T(8,128)(2,1)} %b0), channel_id=1, source_target_pairs={{0,2},{1,3},{2,0},{3,1},{4,6},{5,7},{6,4},{7,5},{8,10},{9,11},{10,... | collective-permute-start | bytes 786440 | tf_op jit(solution)/shard_map/ppermute | solution.py:22
  3.5 20.4 %collective-permute-start.2 = (bf16[128,8,128]{2,1,0:T(8,128)(2,1)}, bf16[128,8,128]{2,1,0:T(8,128)(2,1)}, u32[]{:S(2)}, u32[]{:S(2)}) collective-permute-start(bf16[128,8,128]{2,1,0:T(8,128)(2,1)} %b0), channel_id=1, source_target_pairs={{0,1},{1,2},{2,3},{3,0},{4,5},{5,6},{6,7},{7,4},{8,9},{9,10},{10,1... | collective-permute-start | bytes 786440 | tf_op jit(solution)/shard_map/ppermute | solution.py:22
  5.0 18.8 %collective-permute-start.3 = (f32[512,4,128]{2,1,0:T(4,128)S(1)}, f32[512,4,128]{2,1,0:T(4,128)}, u32[]{:S(2)}, u32[]{:S(2)}) collective-permute-start(f32[512,4,128]{2,1,0:T(4,128)S(1)} %pad_convert_fusion.c_ref.c1), channel_id=1, source_target_pairs={{0,4},{4,8},{8,12},{12,16},{16,20},{20,24},{24,28},{28,32},{32,36}... | collective-permute-start | bytes 3145736 | tf_op jit(solution)/shard_map/ppermute | solution.py:28
  7.0 16.9 %collective-permute-start.4 = (f32[512,4,128]{2,1,0:T(4,128)S(1)}, f32[512,4,128]{2,1,0:T(4,128)}, u32[]{:S(2)}, u32[]{:S(2)}) collective-permute-start(f32[512,4,128]{2,1,0:T(4,128)S(1)} %pad_convert_fusion.c_ref.c1), channel_id=1, source_target_pairs={{4,0},{8,4},{12,8},{16,12},{20,16},{24,20},{28,24},{32,28},{36,32}... | collective-permute-start | bytes 3145736 | tf_op jit(solution)/shard_map/ppermute | solution.py:28
  28.5 35.8 %collective-permute-start.5 = (bf16[512,8,128]{2,1,0:T(8,128)(2,1)}, bf16[512,8,128]{2,1,0:T(8,128)(2,1)}, u32[]{:S(2)}, u32[]{:S(2)}) collective-permute-start(bf16[512,8,128]{2,1,0:T(8,128)(2,1)} %arrange.1.q_ref.q1), channel_id=1, source_target_pairs={{0,4},{4,8},{8,12},{12,16},{16,20},{20,24},{24,28},{28,32},{32,36}... | collective-permute-start | bytes 3145736 | tf_op jit(solution)/shard_map/ppermute | solution.py:28
  33.8 30.5 %collective-permute-start.6 = (bf16[512,8,128]{2,1,0:T(8,128)(2,1)}, bf16[512,8,128]{2,1,0:T(8,128)(2,1)}, u32[]{:S(2)}, u32[]{:S(2)}) collective-permute-start(bf16[512,8,128]{2,1,0:T(8,128)(2,1)} %arrange.1.q_ref.q1), channel_id=1, source_target_pairs={{4,0},{8,4},{12,8},{16,12},{20,16},{24,20},{28,24},{32,28},{36,32}... | collective-permute-start | bytes 3145736 | tf_op jit(solution)/shard_map/ppermute | solution.py:28
  38.3 24.1 %copy-start.12 = (bf16[64,64,64]{2,1,0:T(8,128)(2,1)S(1)}, bf16[64,64,64]{2,1,0:T(8,128)(2,1)}, u32[]{:S(2)}) copy-start(bf16[64,64,64]{2,1,0:T(8,128)(2,1)} %param.27) | copy-start | bytes 1572868
  38.3 25.9 %copy-start.8 = (s32[3]{0:T(128)S(1)}, s32[3]{0:T(128)}, u32[]{:S(2)}) copy-start(s32[3]{0:T(128)} %constant.176.clone.share) | copy-start | bytes 40
  38.3 23.9 %collective-permute-start.7 = (bf16[16,8,64]{2,1,0:T(8,128)(2,1)S(1)}, bf16[16,8,64]{2,1,0:T(8,128)(2,1)S(1)}, u32[]{:S(2)}, u32[]{:S(2)}) collective-permute-start(bf16[16,8,64]{2,1,0:T(8,128)(2,1)S(1)} %fusion.2), channel_id=1, source_target_pairs={{0,3},{1,0},{2,1},{3,2},{4,7},{5,4},{6,5},{7,6},{8,11},{9,8},{10,9... | collective-permute-start | bytes 49160 | tf_op jit(solution)/shard_map/ppermute | solution.py:22
  40.4 21.8 %collective-permute-start.8 = (bf16[16,8,64]{2,1,0:T(8,128)(2,1)S(1)}, bf16[16,8,64]{2,1,0:T(8,128)(2,1)S(1)}, u32[]{:S(2)}, u32[]{:S(2)}) collective-permute-start(bf16[16,8,64]{2,1,0:T(8,128)(2,1)S(1)} %fusion.2), channel_id=1, source_target_pairs={{0,2},{1,3},{2,0},{3,1},{4,6},{5,7},{6,4},{7,5},{8,10},{9,11},{10,... | collective-permute-start | bytes 49160 | tf_op jit(solution)/shard_map/ppermute | solution.py:22
  42.3 20.0 %collective-permute-start.9 = (bf16[16,8,64]{2,1,0:T(8,128)(2,1)S(1)}, bf16[16,8,64]{2,1,0:T(8,128)(2,1)S(1)}, u32[]{:S(2)}, u32[]{:S(2)}) collective-permute-start(bf16[16,8,64]{2,1,0:T(8,128)(2,1)S(1)} %fusion.2), channel_id=1, source_target_pairs={{0,1},{1,2},{2,3},{3,0},{4,5},{5,6},{6,7},{7,4},{8,9},{9,10},{10,1... | collective-permute-start | bytes 49160 | tf_op jit(solution)/shard_map/ppermute | solution.py:22
  63.0 1.2 collective-permute-start.10
  64.2 16.2 %copy-start.7 = (s32[3]{0:T(128)S(1)}, s32[3]{0:T(128)}, u32[]{:S(2)}) copy-start(s32[3]{0:T(128)} %constant.177.clone.share) | copy-start | bytes 40
  74.7 33.0 %collective-permute-start.13 = (bf16[64,8,64]{2,1,0:T(8,128)(2,1)S(1)}, bf16[64,8,64]{2,1,0:T(8,128)(2,1)S(1)}, u32[]{:S(2)}, u32[]{:S(2)}) collective-permute-start(bf16[64,8,64]{2,1,0:T(8,128)(2,1)S(1)} %bitcast.79), channel_id=1, source_target_pairs={{0,4},{4,8},{8,12},{12,16},{16,20},{20,24},{24,28},{28,32},{32,36}... | collective-permute-start | bytes 196616 | tf_op jit(solution)/shard_map/ppermute | solution.py:28
  76.8 30.9 %collective-permute-start.14 = (bf16[64,8,64]{2,1,0:T(8,128)(2,1)S(1)}, bf16[64,8,64]{2,1,0:T(8,128)(2,1)S(1)}, u32[]{:S(2)}, u32[]{:S(2)}) collective-permute-start(bf16[64,8,64]{2,1,0:T(8,128)(2,1)S(1)} %bitcast.80), channel_id=1, source_target_pairs={{4,0},{8,4},{12,8},{16,12},{20,16},{24,20},{28,24},{32,28},{36,32}... | collective-permute-start | bytes 196616 | tf_op jit(solution)/shard_map/ppermute | solution.py:28
  80.3 7.0 %collective-permute-start.11 = (bf16[2,8,64]{2,1,0:T(8,128)(2,1)S(1)}, bf16[2,8,64]{2,1,0:T(8,128)(2,1)S(1)}, u32[]{:S(2)}, u32[]{:S(2)}) collective-permute-start(bf16[2,8,64]{2,1,0:T(8,128)(2,1)S(1)} %pad_maximum_fusion.6), channel_id=1, source_target_pairs={{0,8},{4,12},{8,0},{12,4},{16,24},{20,28},{24,16},{28,20},{32,40},... | collective-permute-start | bytes 6152 | tf_op jit(solution)/shard_map/ppermute | solution.py:412
  87.4 9.0 %collective-permute-start.12 = (bf16[4,8,64]{2,1,0:T(8,128)(2,1)S(1)}, bf16[4,8,64]{2,1,0:T(8,128)(2,1)S(1)}, u32[]{:S(2)}, u32[]{:S(2)}) collective-permute-start(bf16[4,8,64]{2,1,0:T(8,128)(2,1)S(1)} %pad_maximum_fusion.5), channel_id=1, source_target_pairs={{0,16},{4,20},{8,24},{12,28},{16,0},{20,4},{24,8},{28,12},{32,48},... | collective-permute-start | bytes 12296 | tf_op jit(solution)/shard_map/ppermute | solution.py:412
  96.3 15.5 %copy-start.4 = (s32[3]{0:T(128)S(1)}, s32[3]{0:T(128)}, u32[]{:S(2)}) copy-start(s32[3]{0:T(128)} %constant.180.clone.share) | copy-start | bytes 40
  96.4 11.3 %collective-permute-start.15 = (bf16[8,8,64]{2,1,0:T(8,128)(2,1)S(1)}, bf16[8,8,64]{2,1,0:T(8,128)(2,1)S(1)}, u32[]{:S(2)}, u32[]{:S(2)}) collective-permute-start(bf16[8,8,64]{2,1,0:T(8,128)(2,1)S(1)} %pad_maximum_fusion.4), channel_id=1, source_target_pairs={{0,32},{4,36},{8,40},{12,44},{16,48},{20,52},{24,56},{28,60},{32,0... | collective-permute-start | bytes 24584 | tf_op jit(solution)/shard_map/ppermute | solution.py:412
  107.7 17.1 %copy-start.3 = (s32[3]{0:T(128)S(1)}, s32[3]{0:T(128)}, u32[]{:S(2)}) copy-start(s32[3]{0:T(128)} %constant.181.clone.share) | copy-start | bytes 40
  107.7 9.8 %collective-permute-start.16 = (bf16[16,8,64]{2,1,0:T(8,128)(2,1)S(1)}, bf16[16,8,64]{2,1,0:T(8,128)(2,1)S(1)}, u32[]{:S(2)}, u32[]{:S(2)}) collective-permute-start(bf16[16,8,64]{2,1,0:T(8,128)(2,1)S(1)} %pad_maximum_fusion.3), channel_id=1, source_target_pairs={{0,64},{4,68},{8,72},{12,76},{16,80},{20,84},{24,88},{28,92},{32,9... | collective-permute-start | bytes 49160 | tf_op jit(solution)/shard_map/ppermute | solution.py:412
  117.6 18.1 %collective-permute-start.17 = (bf16[32,8,64]{2,1,0:T(8,128)(2,1)S(1)}, bf16[32,8,64]{2,1,0:T(8,128)(2,1)S(1)}, u32[]{:S(2)}, u32[]{:S(2)}) collective-permute-start(bf16[32,8,64]{2,1,0:T(8,128)(2,1)S(1)} %pad_maximum_fusion.2), channel_id=1, source_target_pairs={{0,128},{4,132},{8,136},{12,140},{16,144},{20,148},{24,152},{28,15... | collective-permute-start | bytes 98312 | tf_op jit(solution)/shard_map/ppermute | solution.py:412
  (18 other events, 147.2 us)
where the time goes:
time: 143 us; the launch traced here: 142 us
  Pallas kernels  63.5 us (44%)
  starting transfers between devices  44.3 us (31%)
  local copies, waits for them, and re-layouts  14.6 us (10%)
  matrix products  11.8 us (8%)
  other arithmetic  6.39 us (4%)
    pallas_call x5, Pallas kernels, near_next(): pl.pallas_call(near_next_kernel, out_shape=jax.ShapeDtypeStruct(acc.shape...  31.6 us
    pallas_call x1, Pallas kernels, near_own(): pl.pallas_call(near_own_kernel, out_shape=jax.ShapeDtypeStruct((targets +...  18.8 us
    ppermute x6, starting transfers between devices, slide(): return lax.ppermute(x, axis, pairs)  18.3 us
    ppermute x6, starting transfers between devices, on_device(): other = lax.ppermute(table, 'leaf', [(i, i ^ reach) for i in range(leaves)])  18.2 us
    unnamed x58, local copies, waits for them, and re-layouts  10.1 us
    pallas_call x1, Pallas kernels, near_first(): pl.pallas_call(near_first_kernel, out_shape=(jax.ShapeDtypeStruct(acc.sha...  9.42 us
    ppermute x6, starting transfers between devices, shift(): return lax.ppermute(x, axis, [(i, (i + by) % count) for i in range(count)])  7.74 us
    dot_general x2, matrix products, far_field(): jnp.einsum('bkrc,bkcp->brp', source, couplings, preferred_element_type=jn...  3.83 us
  transfers between devices with their start and end apart: 18, of which 1 were waited for; matrix products, arithmetic and copies ran while one was open for 17% of the time, Pallas kernels for 36%

commit v1 on v0

--- a/solution.py
+++ b/solution.py
@@ -14,6 +14,8 @@
 UNITS = 16
 STRIDE = 32
 CLASSES = (128, 96, 64)
+COSTS = (5, 4, 3)
+OWN_UNITS = 2
 VMEM_LIMIT = 36 << 20
 
 
@@ -33,19 +35,22 @@
     return [x] + [shift(x, axis, -k) for k in range(1, count)]
 
 
-def prepare_targets(low, count, order, own_ref, tile_t):
-    pick = lax.broadcasted_iota(jnp.int32, (8, 384), 1) // 128
-    pick = (pick == lax.broadcasted_iota(jnp.int32, (8, 384), 0)).astype(jnp.bfloat16)
-    targets = own_ref.shape[0]
+def prepare_targets(low, count, order, first, src_c, tile_t):
+    pick = lax.broadcasted_iota(jnp.int32, (8, 256), 1) // 128
+    pick = (pick == lax.broadcasted_iota(jnp.int32, (8, 256), 0)).astype(jnp.bfloat16)
+    line = lax.broadcasted_iota(jnp.int32, (8, 128), 0)
+    targets = order.shape[0]
 
     def body(w, _):
         for j in range(8):
             row = w * 8 + j
-            own = own_ref[order[jnp.minimum(low + row, targets - 1)]]
-            x = jnp.concatenate([own, jnp.zeros((4, 128), jnp.float32)], axis=0)
-            wide = jnp.dot(x.T.astype(jnp.bfloat16), pick, preferred_element_type=jnp.float32)
-            for c in range(3):
-                tile_t[row * 3 + c] = wide[:, 128 * c : 128 * c + 128]
+            at = first + order[jnp.minimum(low + row, targets - 1)]
+            x = [jnp.broadcast_to(src_c[c, pl.ds(at, 1), :], (8, 128)) for c in range(3)]
+            x = jnp.where(line == 0, x[0], jnp.where(line == 1, x[1], x[2])).T
+            wide = jnp.dot(x.astype(jnp.bfloat16), pick, preferred_element_type=jnp.float32)
+            tile_t[row * 3] = wide[:, :128]
+            tile_t[row * 3 + 1] = wide[:, 128:]
+            tile_t[row * 3 + 2] = jnp.broadcast_to(x[:, 2:3], (128, 128))
         return 0
 
     lax.fori_loop(0, (count + 7) // 8, body, 0)
@@ -97,10 +102,24 @@
     )(place, counts, *blocks)
 
 
-def near_steps(plan, low, high, own_ref, tile_t, src_c, src_q, acc, away):
+def split(bounds, part, parts):
+    left = jnp.int32(0)
+    for k, cost in enumerate(COSTS):
+        left = left + (bounds[k + 1] - bounds[k]) * cost
+    left = left * part // parts
+    at = jnp.int32(0)
+    for k, cost in enumerate(COSTS):
+        number = bounds[k + 1] - bounds[k]
+        take = jnp.minimum(left // cost, number)
+        at = at + take
+        left = jnp.where(take == number, left - take * cost, 0)
+    return at
+
+
+def near_steps(plan, low, high, first_own, tile_t, src_c, src_q, acc, away):
     words, lists, bounds, ranks, order = plan
     bf = jnp.bfloat16
-    targets = own_ref.shape[0]
+    targets = order.shape[0]
 
     def rank_of(u):
         return ranks[lax.shift_right_logical(words[u], 5)]
@@ -109,7 +128,7 @@
     some = end > low * UNITS
     base = jnp.where(some, rank_of(jnp.where(some, low * UNITS, 0)), 0)
     count = jnp.where(some, rank_of(jnp.where(some, end - 1, 0)) + 1 - base, 0)
-    prepare_targets(base, count, order, own_ref, tile_t)
+    prepare_targets(base, count, order, first_own, src_c, tile_t)
 
     def unit(word, rows):
         t = lax.shift_right_logical(word, 5)
@@ -123,7 +142,8 @@
         columns = []
         for i in ids:
             source = [
-                jnp.broadcast_to(src_c[i, c : c + 1, :], (16, 128)).astype(bf) for c in range(3)
+                jnp.broadcast_to(src_c[c, pl.ds(i, 1), :], (16, 128)).astype(bf)
+                for c in range(3)
             ]
             pieces = []
             for m in range(rows // 16):
@@ -155,47 +175,50 @@
         lax.fori_loop(first, jnp.maximum(first, last), functools.partial(step, rows), 0)
 
 
-def near_own_kernel(w, l, b, r, o, own_ref, c_ref, q_ref, acc, tile_t, src_c, src_q, sems):
+def spread_coords(planes, src_c):
+    group = planes[0].shape[1]
+    for c in range(3):
+        for k, plane in enumerate(planes):
+            src_c[c, k * group : (k + 1) * group, :] = plane[c].astype(jnp.float32)
+        src_c[c, len(planes) * group :, :] = jnp.zeros((8, 128), jnp.float32)
+
+
+def near_own_kernel(share, w, l, b, r, o, c_ref, q_ref, acc, tile_t, src_c, src_q, sem):
     group = q_ref.shape[0]
+    copy = pltpu.make_async_copy(q_ref, src_q.at[pl.ds(0, group)], sem)
+    copy.start()
+    src_q[group] = jnp.zeros(src_q.shape[1:], src_q.dtype)
+    spread_coords([c_ref], src_c)
+    acc[...] = jnp.zeros_like(acc)
+    copy.wait()
+    near_steps((w, l, b, r, o), 0, b[3], share[3], tile_t, src_c, src_q, acc, group)
+
+
+def near_first_kernel(
+    share, w, l, b, r, o, c0, c1, c2, q0, q1, q2, acc_in, acc, src_c, src_q, tile_t, sems
+):
+    group = q0.shape[0]
     copies = [
-        pltpu.make_async_copy(c_ref, src_c.at[pl.ds(0, group)], sems.at[0]),
-        pltpu.make_async_copy(q_ref, src_q.at[pl.ds(0, group)], sems.at[1]),
+        pltpu.make_async_copy(q, src_q.at[pl.ds(k * group, group)], sems.at[k])
+        for k, q in enumerate((q0, q1, q2))
     ]
     for copy in copies:
         copy.start()
-    src_c[group] = jnp.zeros(src_c.shape[1:], src_c.dtype)
-    src_q[group] = jnp.zeros(src_q.shape[1:], src_q.dtype)
-    acc[...] = jnp.zeros_like(acc)
-    for copy in copies:
-        copy.wait()
-    near_steps((w, l, b, r, o), 0, b[3], own_ref, tile_t, src_c, src_q, acc, group)
-
-
-def near_first_kernel(
-    share, w, l, b, r, o, own_ref, c0, c1, c2, q0, q1, q2, acc_in, acc, src_c, src_q, tile_t, sems
-):
-    group = q0.shape[0]
-    copies = []
-    for k, (c, q) in enumerate(((c0, q0), (c1, q1), (c2, q2))):
-        rows = pl.ds(k * group, group)
-        copies.append(pltpu.make_async_copy(c, src_c.at[rows], sems.at[k, 0]))
-        copies.append(pltpu.make_async_copy(q, src_q.at[rows], sems.at[k, 1]))
-    for copy in copies:
-        copy.start()
-    src_c[3 * group] = jnp.zeros(src_c.shape[1:], src_c.dtype)
     src_q[3 * group] = jnp.zeros(src_q.shape[1:], src_q.dtype)
+    spread_coords([c0, c1, c2], src_c)
     acc[...] = acc_in[...]
     for copy in copies:
         copy.wait()
-    high = b[3] * share[1] // share[2]
-    near_steps((w, l, b, r, o), 0, high, own_ref, tile_t, src_c, src_q, acc, 0)
-
-
-def near_next_kernel(share, w, l, b, r, o, own_ref, src_c, src_q, acc_in, acc, tile_t):
+    high = split(b, share[1], share[2])
+    near_steps((w, l, b, r, o), 0, high, group + share[3], tile_t, src_c, src_q, acc, 0)
+
+
+def near_next_kernel(share, w, l, b, r, o, src_c, src_q, acc_in, acc, tile_t):
+    group = src_q.shape[0] // 3
     acc[...] = acc_in[...]
-    low = b[3] * share[0] // share[2]
-    high = b[3] * share[1] // share[2]
-    near_steps((w, l, b, r, o), low, high, own_ref, tile_t, src_c, src_q, acc, 0)
+    low = split(b, share[0], share[2])
+    high = split(b, share[1], share[2])
+    near_steps((w, l, b, r, o), low, high, group + share[3], tile_t, src_c, src_q, acc, 0)
 
 
 near_params = pltpu.CompilerParams(vmem_limit_bytes=VMEM_LIMIT)
@@ -208,70 +231,163 @@
     return pltpu.VMEM((targets * 3 + 3, 128, 128), jnp.float32)
 
 
-def near_own(plan, own_coords, coords, charges):
+def near_own(share, plan, coords, charges, targets):
     group = charges.shape[0]
-    targets = own_coords.shape[0]
     return pl.pallas_call(
         near_own_kernel,
         out_shape=jax.ShapeDtypeStruct((targets + 1, 8, 128), jnp.float32),
         grid_spec=pltpu.PrefetchScalarGridSpec(
-            num_scalar_prefetch=5,
+            num_scalar_prefetch=6,
             grid=(),
-            in_specs=[in_vmem] + [in_place] * 2,
+            in_specs=[in_vmem, in_place],
             out_specs=in_vmem,
             scratch_shapes=[
                 tile_scratch(targets),
-                pltpu.VMEM((group + 1, 4, 128), jnp.float32),
+                pltpu.VMEM((3, group + 8, 128), jnp.float32),
                 pltpu.VMEM((group + 1, 8, 128), jnp.bfloat16),
-                pltpu.SemaphoreType.DMA((2,)),
+                pltpu.SemaphoreType.DMA,
             ],
         ),
         compiler_params=near_params,
         cost_estimate=near_cost,
         name="near_own",
-    )(*plan, own_coords, coords, charges)
-
-
-def near_first(share, plan, own_coords, coords, charges, acc):
+    )(share, *plan, coords, charges)
+
+
+def near_first(share, plan, coords, charges, acc):
     group = charges[0].shape[0]
     return pl.pallas_call(
         near_first_kernel,
         out_shape=(
             jax.ShapeDtypeStruct(acc.shape, jnp.float32),
-            pltpu.VMEM((3 * group + 1, 4, 128), jnp.float32),
+            pltpu.VMEM((3, 3 * group + 8, 128), jnp.float32),
             pltpu.VMEM((3 * group + 1, 8, 128), jnp.bfloat16),
         ),
         grid_spec=pltpu.PrefetchScalarGridSpec(
             num_scalar_prefetch=6,
             grid=(),
-            in_specs=[in_vmem] + [in_place] * 6 + [in_vmem],
+            in_specs=[in_vmem] * 3 + [in_place] * 3 + [in_vmem],
             out_specs=(in_vmem,) * 3,
-            scratch_shapes=[
-                tile_scratch(own_coords.shape[0]),
-                pltpu.SemaphoreType.DMA((3, 2)),
-            ],
+            scratch_shapes=[tile_scratch(acc.shape[0] - 1), pltpu.SemaphoreType.DMA((3,))],
         ),
         compiler_params=near_params,
         cost_estimate=near_cost,
         name="near_first",
-    )(share, *plan, own_coords, *coords, *charges, acc)
-
-
-def near_next(share, plan, own_coords, src_c, src_q, acc):
+    )(share, *plan, *coords, *charges, acc)
+
+
+def near_next(share, plan, src_c, src_q, acc):
     return pl.pallas_call(
         near_next_kernel,
         out_shape=jax.ShapeDtypeStruct(acc.shape, jnp.float32),
         grid_spec=pltpu.PrefetchScalarGridSpec(
             num_scalar_prefetch=6,
             grid=(),
-            in_specs=[in_vmem] * 4,
+            in_specs=[in_vmem] * 3,
             out_specs=in_vmem,
-            scratch_shapes=[tile_scratch(own_coords.shape[0])],
+            scratch_shapes=[tile_scratch(acc.shape[0] - 1)],
         ),
         compiler_params=near_params,
         cost_estimate=near_cost,
         name="near_next",
-    )(share, *plan, own_coords, src_c, src_q, acc)
+    )(share, *plan, src_c, src_q, acc)
+
+
+def boxes_kernel(picks, left, mine, right, couple, out_ref, table):
+    boxes, rhs, rank = out_ref.shape
+    group = mine.shape[0]
+    slots = picks.shape[0] // boxes
+    for k, ref in enumerate((left, mine, right)):
+        part = ref[...].astype(jnp.float32)
+        table[k * group : (k + 1) * group] = jnp.concatenate([part, part], axis=2)
+    table[3 * group] = jnp.zeros((rhs, 2 * rank), jnp.float32)
+    low = lax.broadcasted_iota(jnp.int32, (rhs, 2 * rank), 1) < rank
+
+    def body(w, _):
+        for j in range(4):
+            b = w * 4 + j
+            total = jnp.zeros((rhs, rank), jnp.float32)
+            for k in range(0, slots, 4):
+                at = [table[picks[b * slots + k + i]] for i in range(4)]
+                lhs = jnp.concatenate(
+                    [jnp.where(low, at[0], at[1]), jnp.where(low, at[2], at[3])], axis=1
+                )
+                rhs_block = couple[pl.ds(b * slots + k, 4)].reshape(4 * rank, rank)
+                total = total + jnp.dot(
+                    lhs.astype(jnp.bfloat16), rhs_block, preferred_element_type=jnp.float32
+                )
+            out_ref[b] = total
+        return 0
+
+    lax.fori_loop(0, boxes // 4, body, 0)
+
+
+def box_field(picks, left, mine, right, couple):
+    boxes, slots, rank, _ = couple.shape
+    rhs = mine.shape[1]
+    return pl.pallas_call(
+        boxes_kernel,
+        out_shape=jax.ShapeDtypeStruct((boxes, rhs, rank), jnp.float32),
+        grid_spec=pltpu.PrefetchScalarGridSpec(
+            num_scalar_prefetch=1,
+            grid=(),
+            in_specs=[in_vmem] * 4,
+            out_specs=in_vmem,
+            scratch_shapes=[pltpu.VMEM((3 * mine.shape[0] + 1, rhs, 2 * rank), jnp.float32)],
+        ),
+        compiler_params=pltpu.CompilerParams(vmem_limit_bytes=12 << 20),
+        cost_estimate=pl.CostEstimate(flops=1 << 24, bytes_accessed=4 << 20, transcendentals=0),
+        name="box_field",
+    )(picks, left, mine, right, couple.reshape(boxes * slots, rank, rank))
+
+
+def down_kernel(flips, counts, share, table, c3, t2, box_far, t1, basis, near, out_ref, local):
+    boxes, rhs, rank = box_far.shape
+    leaves = out_ref.shape[0]
+    bf = jnp.bfloat16
+    across = (((1,), (1,)), ((), ()))
+    top = jnp.zeros((rhs, rank), jnp.float32)
+    for k in range(flips.shape[0]):
+        at = flips[k]
+        source = table[jnp.maximum(at, 0)].astype(jnp.float32)
+        source = jnp.where(at >= 0, source, jnp.zeros_like(source)).astype(bf)
+        top = top + jnp.dot(source, c3[k], preferred_element_type=jnp.float32)
+    top = top.astype(bf)
+    for b in range(boxes):
+        part = lax.dot_general(top, t2[share[0] + b], across, preferred_element_type=jnp.float32)
+        local[b] = (box_far[b] + part).astype(bf)
+    point = lax.broadcasted_iota(jnp.int32, (rhs, 128), 1)
+    fan = leaves // boxes
+
+    def body(w, _):
+        for j in range(2 * fan):
+            t = w * 2 * fan + j
+            moment = lax.dot_general(
+                local[w * 2 + j // fan], t1[t], across, preferred_element_type=jnp.float32
+            ).astype(bf)
+            far = jnp.dot(moment, basis[t], preferred_element_type=jnp.float32)
+            out_ref[t] = jnp.where(point < counts[t], near[t] + far, 0.0)
+        return 0
+
+    lax.fori_loop(0, boxes // 2, body, 0)
+
+
+def go_down(flips, counts, share, table, c3, t2, box_far, t1, basis, near):
+    leaves = counts.shape[0]
+    return pl.pallas_call(
+        down_kernel,
+        out_shape=jax.ShapeDtypeStruct((leaves,) + near.shape[1:], jnp.float32),
+        grid_spec=pltpu.PrefetchScalarGridSpec(
+            num_scalar_prefetch=3,
+            grid=(),
+            in_specs=[in_vmem] * 7,
+            out_specs=in_vmem,
+            scratch_shapes=[pltpu.VMEM(box_far.shape, jnp.bfloat16)],
+        ),
+        compiler_params=pltpu.CompilerParams(vmem_limit_bytes=16 << 20),
+        cost_estimate=pl.CostEstimate(flops=1 << 26, bytes_accessed=5 << 20, transcendentals=0),
+        name="go_down",
+    )(flips, counts, share, table, c3, t2, box_far, t1, basis, near)
 
 
 def order_units(first, number, kind, targets, most):
@@ -308,7 +424,7 @@
     lists = jnp.sum(jnp.where(hit, local[:, None, :] - dummy, 0), axis=2) + dummy
     lists = jnp.pad(lists, ((0, 1), (0, 0)), constant_values=dummy).reshape(-1)
     kind = sum((counts <= rows).astype(jnp.int32) for rows in CLASSES[1:])
-    whole = own_number // SLOTS
+    whole = jnp.minimum(own_number // SLOTS, OWN_UNITS)
     units = (number + SLOTS - 1) // SLOTS
     most = targets * ((slots + SLOTS - 1) // SLOTS) + UNITS
     zero = jnp.zeros_like(whole)
@@ -329,13 +445,6 @@
         ranks,
         order,
     )
-
-
-def far_field(moments, lists, couplings, offset):
-    valid = lists >= 0
-    local = jnp.clip(lists - offset, 0, moments.shape[0] - 1)
-    source = jnp.where(valid[..., None, None], moments[local], jnp.zeros((), moments.dtype))
-    return jnp.einsum("bkrc,bkcp->brp", source, couplings, preferred_element_type=jnp.float32)
 
 
 def on_device(
@@ -366,19 +475,19 @@
     tie = lax.optimization_barrier
 
     blocks = gather_ring(charges, "sub")
+    planes = jnp.transpose(coords, (1, 0, 2))
+    left_c = slide(planes, "leaf", 1)
+    right_c = slide(planes, "leaf", -1)
     own_counts = lax.dynamic_slice_in_dim(counts, start, leaf_dev, 0)
-    wide = jnp.pad(coords.astype(jnp.float32), ((0, 0), (0, 1), (0, 0)))
-    left_c = slide(wide, "leaf", 1)
-    right_c = slide(wide, "leaf", -1)
-    own_coords = lax.dynamic_slice_in_dim(wide, start, leaf_dev, 0)
 
     slot = jnp.arange(group_size, dtype=jnp.int32)
     inverse = jnp.sum(jnp.where(morton[None, :] == slot[:, None], slot[None, :], 0), axis=1)
     place = lax.rem(inverse // leaf_dev - lane + lanes, lanes) * leaf_dev + inverse % leaf_dev
     plan_own, plan_all = plan_near(near_list, (group - 1) * group_size, group_size, own_counts)
 
-    blocks, left_c, right_c, plan_own, plan_all = tie((blocks, left_c, right_c, plan_own, plan_all))
+    blocks, plan_own, plan_all = tie((blocks, plan_own, plan_all))
     mine = arrange(place, counts, blocks)
+    mine, left_c, right_c = tie((mine, left_c, right_c))
     left_q = slide(mine, "leaf", 1)
     right_q = slide(mine, "leaf", -1)
 
@@ -394,9 +503,14 @@
         preferred_element_type=jnp.float32,
     ).astype(jnp.bfloat16)
 
+    rounds = (leaves.bit_length() - 1) // 2
+
+    def share_of(k):
+        return jnp.stack([jnp.int32(k), jnp.int32(k + 1), jnp.int32(rounds), start])
+
     mine_after, box_moments = tie((mine, box_moments))
     ring = gather_ring(box_moments, "sub")
-    acc = near_own(plan_own, own_coords, wide, mine_after)
+    acc = near_own(share_of(0), plan_own, planes, mine_after, leaf_dev)
     ring, acc = tie((ring, acc))
     group_moments = jnp.roll(jnp.stack(ring), lane, axis=0)
     group_moments = group_moments.reshape(group_boxes, rhs_count, rank_size)
@@ -404,43 +518,45 @@
         "brc,bcp->rp", group_moments, transfer2, preferred_element_type=jnp.float32
     ).astype(jnp.bfloat16)
 
+    far2_local = jnp.clip(far2_list - (group - 1) * group_boxes, 0, 3 * group_boxes - 1)
+    picks = jnp.where(far2_list >= 0, far2_local, 3 * group_boxes).reshape(-1)
     table = top_moment[None]
-    reach, rounds = 1, (leaves - 1).bit_length()
+    box_far = None
     for k in range(rounds):
-        share = jnp.asarray([k, k + 1, rounds], jnp.int32)
-        table, acc, group_moments = tie((table, acc, group_moments))
-        other = lax.ppermute(table, "leaf", [(i, i ^ reach) for i in range(leaves)])
+        if k == rounds - 1:
+            table, acc, box_far = tie((table, acc, box_far))
+        else:
+            table, acc = tie((table, acc))
+        others = [
+            lax.ppermute(table, "leaf", [(i, i ^ (m << 2 * k)) for i in range(leaves)])
+            for m in (1, 2, 3)
+        ]
         if k == 0:
-            acc, src_c, src_q = near_first(
-                share, plan_all, own_coords, (left_c, wide, right_c), (left_q, mine, right_q), acc
-            )
-        else:
-            acc = near_next(share, plan_all, own_coords, src_c, src_q, acc)
-        if k == 1:
             left_b = slide(group_moments, "leaf", 1)
             right_b = slide(group_moments, "leaf", -1)
-        if k == 3:
-            table, left_b, right_b = tie((table, left_b, right_b))
-        table = jnp.concatenate([table, other], axis=0)
-        reach *= 2
-    flipped = jnp.where(far3_list >= 0, far3_list ^ group, -1)
-    top_field = far_field(table, flipped, coupling3, 0).astype(jnp.bfloat16)
-
-    near_boxes = jnp.concatenate([left_b, group_moments, right_b], axis=0)
-    box_far = far_field(near_boxes, far2_list, coupling2, (group - 1) * group_boxes)
-    own_transfer = lax.dynamic_slice_in_dim(transfer2, lane * clusters, clusters, 0)
-    box_local = (
-        box_far
-        + jnp.einsum("rp,bcp->brc", top_field[0], own_transfer, preferred_element_type=jnp.float32)
-    ).astype(jnp.bfloat16)
-    leaf_local = jnp.einsum(
-        "brp,bncp->bnrc", box_local, transfer_boxed, preferred_element_type=jnp.float32
-    ).astype(jnp.bfloat16)
-    leaf_local = leaf_local.reshape(leaf_dev, rhs_count, rank_size)
-    far_part = jnp.einsum("trk,tkp->trp", leaf_local, basis, preferred_element_type=jnp.float32)
-    point = jnp.arange(points, dtype=jnp.int32)
-    own_live = point[None, :] < own_counts[:, None]
-    return jnp.where(own_live[:, None, :], acc[:leaf_dev] + far_part, jnp.zeros((), jnp.float32))
+            acc, src_c, src_q = near_first(
+                share_of(k), plan_all, (left_c, planes, right_c), (left_q, mine, right_q), acc
+            )
+            others, left_b, right_b, acc = tie((others, left_b, right_b, acc))
+        else:
+            acc = near_next(share_of(k), plan_all, src_c, src_q, acc)
+        if k == 1:
+            box_far = box_field(picks, left_b, group_moments, right_b, coupling2)
+        table = jnp.concatenate([table] + list(others), axis=0)
+    flips = jnp.where(far3_list[0] >= 0, far3_list[0] ^ group, -1)
+    lane_box = (lane * clusters)[None]
+    return go_down(
+        flips,
+        own_counts,
+        lane_box,
+        table,
+        coupling3[0],
+        transfer2,
+        box_far,
+        transfer1,
+        basis,
+        acc,
+    )
 
 
 def solution(mesh):

time: 143 us -> 144 us (level)
  the two profiles are of different devices: /device:TPU:22 before, /device:TPU:1 now
where the time goes in v1:
time: 144 us; the launch traced here: 142 us
  Pallas kernels  76.6 us (53%)
  starting transfers between devices  49.8 us (35%)
  other arithmetic  7.43 us (5%)
  local copies, waits for them, and re-layouts  5.56 us (4%)
  matrix products  1.94 us (1%)
    pallas_call x2, Pallas kernels, near_next(): pl.pallas_call(near_next_kernel, out_shape=jax.ShapeDtypeStruct(acc.shape...  24.1 us
    ppermute x9, starting transfers between devices, on_device(): lax.ppermute(table, 'leaf', [(i, i ^ m << 2 * k) for i in range(leaves)])  23.4 us
    pallas_call x1, Pallas kernels, go_down(): pl.pallas_call(down_kernel, out_shape=jax.ShapeDtypeStruct((leaves,) + ne...  19.5 us
    ppermute x6, starting transfers between devices, slide(): return lax.ppermute(x, axis, pairs)  18.3 us
    pallas_call x1, Pallas kernels, near_own(): pl.pallas_call(near_own_kernel, out_shape=jax.ShapeDtypeStruct((targets +...  17.4 us
    pallas_call x1, Pallas kernels, near_first(): pl.pallas_call(near_first_kernel, out_shape=(jax.ShapeDtypeStruct(acc.sha...  12.3 us
    ppermute x6, starting transfers between devices, shift(): return lax.ppermute(x, axis, [(i, (i + by) % count) for i in range(count)])  8.07 us
    unnamed x23, local copies, waits for them, and re-layouts  4.13 us
  transfers between devices with their start and end apart: 21, of which 0 were waited for; matrix products, arithmetic and copies ran while one was open for 9% of the time, Pallas kernels for 40%

profile of v1, /device:TPU:1, one launch (start us, length us, event | category | flops | bytes accessed | tf_op | source)
XLA Modules:
  0.0 141.9 jit_solution(13881591778594091235)
XLA Ops:
  0.0 3.6 %collective-permute-start = (bf16[128,8,128]{2,1,0:T(8,128)(2,1)}, bf16[128,8,128]{2,1,0:T(8,128)(2,1)S(1)}, u32[]{:S(2)}, u32[]{:S(2)}) collective-permute-start(bf16[128,8,128]{2,1,0:T(8,128)(2,1)} %b0), channel_id=1, source_target_pairs={{0,3},{1,0},{2,1},{3,2},{4,7},{5,4},{6,5},{7,6},{8,11},{9,8},{10,9... | collective-permute-start | bytes 786440 | tf_op jit(solution)/shard_map/ppermute | solution.py:24
  4.6 4.5 %collective-permute-start.3 = (bf16[3,512,128]{2,1,0:T(8,128)(2,1)}, bf16[3,512,128]{2,1,0:T(8,128)(2,1)}, u32[]{:S(2)}, u32[]{:S(2)}) collective-permute-start(bf16[3,512,128]{2,1,0:T(8,128)(2,1)} %bitcast.47), channel_id=1, source_target_pairs={{0,4},{4,8},{8,12},{12,16},{16,20},{20,24},{24,28},{28,32},{32,36}... | collective-permute-start | bytes 1179656 | tf_op jit(solution)/shard_map/ppermute | solution.py:30
  9.1 1.9 %collective-permute-start.4 = (bf16[3,512,128]{2,1,0:T(8,128)(2,1)}, bf16[3,512,128]{2,1,0:T(8,128)(2,1)}, u32[]{:S(2)}, u32[]{:S(2)}) collective-permute-start(bf16[3,512,128]{2,1,0:T(8,128)(2,1)} %bitcast.48), channel_id=1, source_target_pairs={{4,0},{8,4},{12,8},{16,12},{20,16},{24,20},{28,24},{32,28},{36,32}... | collective-permute-start | bytes 1179656 | tf_op jit(solution)/shard_map/ppermute | solution.py:30
  19.9 3.9 %copy.26.t1 = bf16[128,64,64]{2,1,0:T(8,128)(2,1)S(1)} copy(bf16[128,64,64]{0,2,1:T(8,128)(2,1)} %param.18) | data formatting | bytes 2097152 | tf_op args[6]
  24.0 1.6 %arrange.1.q_ref.q1 = bf16[512,8,128]{2,1,0:T(8,128)(2,1)S(1)} custom-call(s32[512]{0:T(512)S(1)} %fusion.16.place, s32[512]{0:T(512)S(1)} %copy-done.5, bf16[128,8,128]{2,1,0:T(8,128)(2,1)S(1)} %copy-done.3, bf16[128,8,128]{2,1,0:T(8,128)(2,1)S(1)} %collective-permute-done.b1, bf16[128,8,128]{2,1,0:T(8,128)(2,1)S(1)} %collective-permute-done.1.b2, ...), custom_call_target="tpu_custom_call" | custom-call | flops 1048576 | bytes 2097152 | tf_op jit(solution)/shard_map/arrange/pallas_call | solution.py:86
  25.7 1.2 convolution_convert_fusion
  27.3 2.1 %collective-permute-start.5 = (bf16[16,8,64]{2,1,0:T(8,128)(2,1)S(1)}, bf16[16,8,64]{2,1,0:T(8,128)(2,1)S(1)}, u32[]{:S(2)}, u32[]{:S(2)}) collective-permute-start(bf16[16,8,64]{2,1,0:T(8,128)(2,1)S(1)} %fusion), channel_id=1, source_target_pairs={{0,3},{1,0},{2,1},{3,2},{4,7},{5,4},{6,5},{7,6},{8,11},{9,8},{10,9... | collective-permute-start | bytes 49160 | tf_op jit(solution)/shard_map/ppermute | solution.py:24
  29.4 1.4 collective-permute-start.6
  30.8 4.2 %collective-permute-start.13 = (bf16[512,8,128]{2,1,0:T(8,128)(2,1)S(1)}, bf16[512,8,128]{2,1,0:T(8,128)(2,1)S(1)}, u32[]{:S(2)}, u32[]{:S(2)}) collective-permute-start(bf16[512,8,128]{2,1,0:T(8,128)(2,1)S(1)} %arrange.1.q_ref.q1), channel_id=1, source_target_pairs={{0,4},{4,8},{8,12},{12,16},{16,20},{20,24},{24,28},{28,32},{32,36}... | collective-permute-start | bytes 3145736 | tf_op jit(solution)/shard_map/ppermute | solution.py:30
  35.0 1.9 %collective-permute-start.14 = (bf16[512,8,128]{2,1,0:T(8,128)(2,1)S(1)}, bf16[512,8,128]{2,1,0:T(8,128)(2,1)S(1)}, u32[]{:S(2)}, u32[]{:S(2)}) collective-permute-start(bf16[512,8,128]{2,1,0:T(8,128)(2,1)S(1)} %arrange.1.q_ref.q1), channel_id=1, source_target_pairs={{4,0},{8,4},{12,8},{16,12},{20,16},{24,20},{28,24},{32,28},{36,32}... | collective-permute-start | bytes 3145736 | tf_op jit(solution)/shard_map/ppermute | solution.py:30
  36.9 17.4 %near_own.1.acc_in = f32[129,8,128]{2,1,0:T(8,128)S(1)} custom-call(s32[4]{0:T(128)S(1)} %fusion.19.share, s32[912]{0:T(1024)S(1)} %get-tuple-element.51.w, s32[4128]{0:T(1024)S(1)} %compare_select_fusion.l, s32[5]{0:T(128)S(1)} %fusion.21.b, s32[129]{0:T(256)S(1)} %pad.9.r, s32[128]{0:T(128)S(1)} %select_reduce_fusion.5.o, ...), custom_call_target="tpu_custom_call" | custom-call | flops 4294967296 | bytes 1048576 | tf_op jit(solution)/shard_map/near_own/pallas_call | solution.py:236
  54.5 3.8 %collective-permute-start.11 = (bf16[64,8,64]{2,1,0:T(8,128)(2,1)S(1)}, bf16[64,8,64]{2,1,0:T(8,128)(2,1)S(1)}, u32[]{:S(2)}, u32[]{:S(2)}) collective-permute-start(bf16[64,8,64]{2,1,0:T(8,128)(2,1)S(1)} %bitcast.42), channel_id=1, source_target_pairs={{0,4},{4,8},{8,12},{12,16},{16,20},{20,24},{24,28},{28,32},{32,36}... | collective-permute-start | bytes 196616 | tf_op jit(solution)/shard_map/ppermute | solution.py:30
  58.3 1.9 %collective-permute-start.12 = (bf16[64,8,64]{2,1,0:T(8,128)(2,1)S(1)}, bf16[64,8,64]{2,1,0:T(8,128)(2,1)S(1)}, u32[]{:S(2)}, u32[]{:S(2)}) collective-permute-start(bf16[64,8,64]{2,1,0:T(8,128)(2,1)S(1)} %bitcast.43), channel_id=1, source_target_pairs={{4,0},{8,4},{12,8},{16,12},{20,16},{24,20},{28,24},{32,28},{36,32}... | collective-permute-start | bytes 196616 | tf_op jit(solution)/shard_map/ppermute | solution.py:30
  60.5 2.0 %collective-permute-start.10 = (bf16[1,8,64]{2,1,0:T(8,128)(2,1)S(1)}, bf16[1,8,64]{2,1,0:T(8,128)(2,1)S(1)}, u32[]{:S(2)}, u32[]{:S(2)}) collective-permute-start(bf16[1,8,64]{2,1,0:T(8,128)(2,1)S(1)} %fusion.2), channel_id=1, source_target_pairs={{0,12},{4,8},{8,4},{12,0},{16,28},{20,24},{24,20},{28,16},{32,44},... | collective-permute-start | bytes 3080 | tf_op jit(solution)/shard_map/ppermute | solution.py:531
  62.8 12.3 %near_first.1 = (f32[129,8,128]{2,1,0:T(8,128)S(1)}, f32[3,1544,128]{2,1,0:T(8,128)S(1)}, bf16[1537,8,128]{2,1,0:T(8,128)(2,1)S(1)}) custom-call(s32[4]{0:T(128)S(1)} %fusion.19.share, s32[912]{0:T(1024)S(1)} %get-tuple-element.63.w, s32[4128]{0:T(1024)S(1)} %reshape.92.l, s32[5]{0:T(128)S(1)} %fusion.22.b, s32[129]{0:T(256)S(1)} %pad.9.r, ...), custom_call_target="tpu_custom_call" | custom-call | flops 4294967296 | bytes 1048576 | tf_op jit(solution)/shard_map/near_first/pallas_call | solution.py:259
  75.2 6.1 %collective-permute-start.15 = (bf16[4,8,64]{2,1,0:T(8,128)(2,1)S(1)}, bf16[4,8,64]{2,1,0:T(8,128)(2,1)S(1)}, u32[]{:S(2)}, u32[]{:S(2)}) collective-permute-start(bf16[4,8,64]{2,1,0:T(8,128)(2,1)S(1)} %pad_maximum_fusion.2), channel_id=1, source_target_pairs={{0,16},{4,20},{8,24},{12,28},{16,0},{20,4},{24,8},{28,12},{32,48},... | collective-permute-start | bytes 12296 | tf_op jit(solution)/shard_map/ppermute | solution.py:531
  81.2 2.9 %collective-permute-start.16 = (bf16[4,8,64]{2,1,0:T(8,128)(2,1)S(1)}, bf16[4,8,64]{2,1,0:T(8,128)(2,1)S(1)}, u32[]{:S(2)}, u32[]{:S(2)}) collective-permute-start(bf16[4,8,64]{2,1,0:T(8,128)(2,1)S(1)} %pad_maximum_fusion.2), channel_id=1, source_target_pairs={{0,32},{4,36},{8,40},{12,44},{16,48},{20,52},{24,56},{28,60},{32,0... | collective-permute-start | bytes 12296 | tf_op jit(solution)/shard_map/ppermute | solution.py:531
  84.2 2.6 %collective-permute-start.17 = (bf16[4,8,64]{2,1,0:T(8,128)(2,1)S(1)}, bf16[4,8,64]{2,1,0:T(8,128)(2,1)S(1)}, u32[]{:S(2)}, u32[]{:S(2)}) collective-permute-start(bf16[4,8,64]{2,1,0:T(8,128)(2,1)S(1)} %pad_maximum_fusion.2), channel_id=1, source_target_pairs={{0,48},{4,52},{8,56},{12,60},{16,32},{20,36},{24,40},{28,44},{32,1... | collective-permute-start | bytes 12296 | tf_op jit(solution)/shard_map/ppermute | solution.py:531
  86.8 11.7 %near_next.2.acc_in = f32[129,8,128]{2,1,0:T(8,128)S(1)} custom-call(s32[4]{0:T(128)S(1)} %fusion.20.share, s32[912]{0:T(1024)S(1)} %get-tuple-element.63.w, s32[4128]{0:T(1024)S(1)} %reshape.92.l, s32[5]{0:T(128)S(1)} %fusion.22.b, s32[129]{0:T(256)S(1)} %pad.9.r, s32[128]{0:T(128)S(1)} %select_reduce_fusion.5.o, ...), custom_call_target="tpu_custom_call" | custom-call | flops 4294967296 | bytes 1048576 | tf_op jit(solution)/shard_map/near_next/pallas_call | solution.py:280
  98.4 1.7 %box_field.1.box_far = f32[16,8,64]{2,1,0:T(8,128)S(1)} custom-call(s32[256]{0:T(256)S(1)} %reshape.96.picks, bf16[64,8,64]{2,1,0:T(8,128)(2,1)S(1)} %collective-permute-done.11.left, bf16[64,8,64]{2,1,0:T(8,128)(2,1)S(1)} %bitcast.45, bf16[64,8,64]{2,1,0:T(8,128)(2,1)S(1)} %collective-permute-done.12.right, bf16[256,64,64]{2,1,0:T(8,128)(2,1)S(1)} %bitcast.41), custom_call_target="tpu_custom_call" | custom-call | flops 16777216 | bytes 4194304 | tf_op jit(solution)/shard_map/box_field/pallas_call | solution.py:328
  100.2 3.6 %collective-permute-start.18 = (bf16[16,8,64]{2,1,0:T(8,128)(2,1)S(1)}, bf16[16,8,64]{2,1,0:T(8,128)(2,1)S(1)}, u32[]{:S(2)}, u32[]{:S(2)}) collective-permute-start(bf16[16,8,64]{2,1,0:T(8,128)(2,1)S(1)} %pad_maximum_fusion.1), channel_id=1, source_target_pairs={{0,64},{4,68},{8,72},{12,76},{16,80},{20,84},{24,88},{28,92},{32,9... | collective-permute-start | bytes 49160 | tf_op jit(solution)/shard_map/ppermute | solution.py:531
  103.8 5.9 %collective-permute-start.19 = (bf16[16,8,64]{2,1,0:T(8,128)(2,1)S(1)}, bf16[16,8,64]{2,1,0:T(8,128)(2,1)S(1)}, u32[]{:S(2)}, u32[]{:S(2)}) collective-permute-start(bf16[16,8,64]{2,1,0:T(8,128)(2,1)S(1)} %pad_maximum_fusion.1), channel_id=1, source_target_pairs={{0,128},{4,132},{8,136},{12,140},{16,144},{20,148},{24,152},{28,15... | collective-permute-start | bytes 49160 | tf_op jit(solution)/shard_map/ppermute | solution.py:531
  109.9 12.4 %near_next.3.near = f32[129,8,128]{2,1,0:T(8,128)S(1)} custom-call(s32[4]{0:T(128)S(1)} %add_add_fusion.share, s32[912]{0:T(1024)S(1)} %get-tuple-element.63.w, s32[4128]{0:T(1024)S(1)} %reshape.92.l, s32[5]{0:T(128)S(1)} %fusion.22.b, s32[129]{0:T(256)S(1)} %pad.9.r, s32[128]{0:T(128)S(1)} %select_reduce_fusion.5.o, ...), custom_call_target="tpu_custom_call" | custom-call | flops 4294967296 | bytes 1048576 | tf_op jit(solution)/shard_map/near_next/pallas_call | solution.py:280
  122.4 19.5 %go_down.1 = f32[128,8,128]{2,1,0:T(8,128)} custom-call(s32[8]{0:T(128)S(1)} %fusion.23.flips, s32[128]{0:T(128)S(1)} %get-tuple-element.97.counts, s32[1]{0:T(128)} %bitcast.1.share, bf16[64,8,64]{2,1,0:T(8,128)(2,1)S(1)} %pad_maximum_fusion.table, bf16[8,64,64]{2,1,0:T(8,128)(2,1)S(1)} %bitcast.46, bf16[64,64,64]{2,1,0:T(8,128)(2,1)S(1)} %copy-done.1, ...), custom_call_target="tpu_custom_call" | custom-call | flops 67108864 | bytes 5242880 | tf_op jit(solution)/shard_map/go_down/pallas_call | solution.py:377
  (90 shorter events, 11.3 us)
Async XLA Ops:
  0.0 24.0 %copy-start.3 = (bf16[128,8,128]{2,1,0:T(8,128)(2,1)S(1)}, bf16[128,8,128]{2,1,0:T(8,128)(2,1)}, u32[]{:S(2)}) copy-start(bf16[128,8,128]{2,1,0:T(8,128)(2,1)} %b0) | copy-start | bytes 786436
  0.0 24.0 %copy-start.5 = (s32[512]{0:T(512)S(1)}, s32[512]{0:T(512)}, u32[]{:S(2)}) copy-start(s32[512]{0:T(512)} %counts.1) | copy-start | bytes 6148
  0.0 24.0 %collective-permute-start = (bf16[128,8,128]{2,1,0:T(8,128)(2,1)}, bf16[128,8,128]{2,1,0:T(8,128)(2,1)S(1)}, u32[]{:S(2)}, u32[]{:S(2)}) collective-permute-start(bf16[128,8,128]{2,1,0:T(8,128)(2,1)} %b0), channel_id=1, source_target_pairs={{0,3},{1,0},{2,1},{3,2},{4,7},{5,4},{6,5},{7,6},{8,11},{9,8},{10,9... | collective-permute-start | bytes 786440 | tf_op jit(solution)/shard_map/ppermute | solution.py:24
  3.6 20.4 %collective-permute-start.1 = (bf16[128,8,128]{2,1,0:T(8,128)(2,1)}, bf16[128,8,128]{2,1,0:T(8,128)(2,1)S(1)}, u32[]{:S(2)}, u32[]{:S(2)}) collective-permute-start(bf16[128,8,128]{2,1,0:T(8,128)(2,1)} %b0), channel_id=1, source_target_pairs={{0,2},{1,3},{2,0},{3,1},{4,6},{5,7},{6,4},{7,5},{8,10},{9,11},{10,... | collective-permute-start | bytes 786440 | tf_op jit(solution)/shard_map/ppermute | solution.py:24
  3.9 20.1 %collective-permute-start.2 = (bf16[128,8,128]{2,1,0:T(8,128)(2,1)}, bf16[128,8,128]{2,1,0:T(8,128)(2,1)S(1)}, u32[]{:S(2)}, u32[]{:S(2)}) collective-permute-start(bf16[128,8,128]{2,1,0:T(8,128)(2,1)} %b0), channel_id=1, source_target_pairs={{0,1},{1,2},{2,3},{3,0},{4,5},{5,6},{6,7},{7,4},{8,9},{9,10},{10,1... | collective-permute-start | bytes 786440 | tf_op jit(solution)/shard_map/ppermute | solution.py:24
  4.6 21.0 %collective-permute-start.3 = (bf16[3,512,128]{2,1,0:T(8,128)(2,1)}, bf16[3,512,128]{2,1,0:T(8,128)(2,1)}, u32[]{:S(2)}, u32[]{:S(2)}) collective-permute-start(bf16[3,512,128]{2,1,0:T(8,128)(2,1)} %bitcast.47), channel_id=1, source_target_pairs={{0,4},{4,8},{8,12},{12,16},{16,20},{20,24},{24,28},{28,32},{32,36}... | collective-permute-start | bytes 1179656 | tf_op jit(solution)/shard_map/ppermute | solution.py:30
  9.1 16.5 %collective-permute-start.4 = (bf16[3,512,128]{2,1,0:T(8,128)(2,1)}, bf16[3,512,128]{2,1,0:T(8,128)(2,1)}, u32[]{:S(2)}, u32[]{:S(2)}) collective-permute-start(bf16[3,512,128]{2,1,0:T(8,128)(2,1)} %bitcast.48), channel_id=1, source_target_pairs={{4,0},{8,4},{12,8},{16,12},{20,16},{24,20},{28,24},{32,28},{36,32}... | collective-permute-start | bytes 1179656 | tf_op jit(solution)/shard_map/ppermute | solution.py:30
  27.3 32.9 %copy-start.1 = (bf16[64,64,64]{2,1,0:T(8,128)(2,1)S(1)}, bf16[64,64,64]{2,1,0:T(8,128)(2,1)}, u32[]{:S(2)}) copy-start(bf16[64,64,64]{2,1,0:T(8,128)(2,1)} %t2.1) | copy-start | bytes 1572868
  27.3 27.0 %collective-permute-start.5 = (bf16[16,8,64]{2,1,0:T(8,128)(2,1)S(1)}, bf16[16,8,64]{2,1,0:T(8,128)(2,1)S(1)}, u32[]{:S(2)}, u32[]{:S(2)}) collective-permute-start(bf16[16,8,64]{2,1,0:T(8,128)(2,1)S(1)} %fusion), channel_id=1, source_target_pairs={{0,3},{1,0},{2,1},{3,2},{4,7},{5,4},{6,5},{7,6},{8,11},{9,8},{10,9... | collective-permute-start | bytes 49160 | tf_op jit(solution)/shard_map/ppermute | solution.py:24
  29.4 24.9 %collective-permute-start.6 = (bf16[16,8,64]{2,1,0:T(8,128)(2,1)S(1)}, bf16[16,8,64]{2,1,0:T(8,128)(2,1)S(1)}, u32[]{:S(2)}, u32[]{:S(2)}) collective-permute-start(bf16[16,8,64]{2,1,0:T(8,128)(2,1)S(1)} %fusion), channel_id=1, source_target_pairs={{0,2},{1,3},{2,0},{3,1},{4,6},{5,7},{6,4},{7,5},{8,10},{9,11},{10,... | collective-permute-start | bytes 49160 | tf_op jit(solution)/shard_map/ppermute | solution.py:24
  30.8 23.5 %collective-permute-start.7 = (bf16[16,8,64]{2,1,0:T(8,128)(2,1)S(1)}, bf16[16,8,64]{2,1,0:T(8,128)(2,1)S(1)}, u32[]{:S(2)}, u32[]{:S(2)}) collective-permute-start(bf16[16,8,64]{2,1,0:T(8,128)(2,1)S(1)} %fusion), channel_id=1, source_target_pairs={{0,1},{1,2},{2,3},{3,0},{4,5},{5,6},{6,7},{7,4},{8,9},{9,10},{10,1... | collective-permute-start | bytes 49160 | tf_op jit(solution)/shard_map/ppermute | solution.py:24
  30.8 31.8 %collective-permute-start.13 = (bf16[512,8,128]{2,1,0:T(8,128)(2,1)S(1)}, bf16[512,8,128]{2,1,0:T(8,128)(2,1)S(1)}, u32[]{:S(2)}, u32[]{:S(2)}) collective-permute-start(bf16[512,8,128]{2,1,0:T(8,128)(2,1)S(1)} %arrange.1.q_ref.q1), channel_id=1, source_target_pairs={{0,4},{4,8},{8,12},{12,16},{16,20},{20,24},{24,28},{28,32},{32,36}... | collective-permute-start | bytes 3145736 | tf_op jit(solution)/shard_map/ppermute | solution.py:30
  35.0 27.6 %collective-permute-start.14 = (bf16[512,8,128]{2,1,0:T(8,128)(2,1)S(1)}, bf16[512,8,128]{2,1,0:T(8,128)(2,1)S(1)}, u32[]{:S(2)}, u32[]{:S(2)}) collective-permute-start(bf16[512,8,128]{2,1,0:T(8,128)(2,1)S(1)} %arrange.1.q_ref.q1), channel_id=1, source_target_pairs={{4,0},{8,4},{12,8},{16,12},{20,16},{24,20},{28,24},{32,28},{36,32}... | collective-permute-start | bytes 3145736 | tf_op jit(solution)/shard_map/ppermute | solution.py:30
  54.5 20.7 %collective-permute-start.11 = (bf16[64,8,64]{2,1,0:T(8,128)(2,1)S(1)}, bf16[64,8,64]{2,1,0:T(8,128)(2,1)S(1)}, u32[]{:S(2)}, u32[]{:S(2)}) collective-permute-start(bf16[64,8,64]{2,1,0:T(8,128)(2,1)S(1)} %bitcast.42), channel_id=1, source_target_pairs={{0,4},{4,8},{8,12},{12,16},{16,20},{20,24},{24,28},{28,32},{32,36}... | collective-permute-start | bytes 196616 | tf_op jit(solution)/shard_map/ppermute | solution.py:30
  58.3 16.9 %collective-permute-start.12 = (bf16[64,8,64]{2,1,0:T(8,128)(2,1)S(1)}, bf16[64,8,64]{2,1,0:T(8,128)(2,1)S(1)}, u32[]{:S(2)}, u32[]{:S(2)}) collective-permute-start(bf16[64,8,64]{2,1,0:T(8,128)(2,1)S(1)} %bitcast.43), channel_id=1, source_target_pairs={{4,0},{8,4},{12,8},{16,12},{20,16},{24,20},{28,24},{32,28},{36,32}... | collective-permute-start | bytes 196616 | tf_op jit(solution)/shard_map/ppermute | solution.py:30
  60.5 14.6 %collective-permute-start.10 = (bf16[1,8,64]{2,1,0:T(8,128)(2,1)S(1)}, bf16[1,8,64]{2,1,0:T(8,128)(2,1)S(1)}, u32[]{:S(2)}, u32[]{:S(2)}) collective-permute-start(bf16[1,8,64]{2,1,0:T(8,128)(2,1)S(1)} %fusion.2), channel_id=1, source_target_pairs={{0,12},{4,8},{8,4},{12,0},{16,28},{20,24},{24,20},{28,16},{32,44},... | collective-permute-start | bytes 3080 | tf_op jit(solution)/shard_map/ppermute | solution.py:531
  62.5 12.6 %collective-permute-start.8 = (bf16[1,8,64]{2,1,0:T(8,128)(2,1)S(1)}, bf16[1,8,64]{2,1,0:T(8,128)(2,1)S(1)}, u32[]{:S(2)}, u32[]{:S(2)}) collective-permute-start(bf16[1,8,64]{2,1,0:T(8,128)(2,1)S(1)} %fusion.2), channel_id=1, source_target_pairs={{0,4},{4,0},{8,12},{12,8},{16,20},{20,16},{24,28},{28,24},{32,36},... | collective-permute-start | bytes 3080 | tf_op jit(solution)/shard_map/ppermute | solution.py:531
  62.5 12.6 %collective-permute-start.9 = (bf16[1,8,64]{2,1,0:T(8,128)(2,1)S(1)}, bf16[1,8,64]{2,1,0:T(8,128)(2,1)S(1)}, u32[]{:S(2)}, u32[]{:S(2)}) collective-permute-start(bf16[1,8,64]{2,1,0:T(8,128)(2,1)S(1)} %fusion.2), channel_id=1, source_target_pairs={{0,8},{4,12},{8,0},{12,4},{16,24},{20,28},{24,16},{28,20},{32,40},... | collective-permute-start | bytes 3080 | tf_op jit(solution)/shard_map/ppermute | solution.py:531
  75.2 25.0 %collective-permute-start.15 = (bf16[4,8,64]{2,1,0:T(8,128)(2,1)S(1)}, bf16[4,8,64]{2,1,0:T(8,128)(2,1)S(1)}, u32[]{:S(2)}, u32[]{:S(2)}) collective-permute-start(bf16[4,8,64]{2,1,0:T(8,128)(2,1)S(1)} %pad_maximum_fusion.2), channel_id=1, source_target_pairs={{0,16},{4,20},{8,24},{12,28},{16,0},{20,4},{24,8},{28,12},{32,48},... | collective-permute-start | bytes 12296 | tf_op jit(solution)/shard_map/ppermute | solution.py:531
  81.2 18.9 %collective-permute-start.16 = (bf16[4,8,64]{2,1,0:T(8,128)(2,1)S(1)}, bf16[4,8,64]{2,1,0:T(8,128)(2,1)S(1)}, u32[]{:S(2)}, u32[]{:S(2)}) collective-permute-start(bf16[4,8,64]{2,1,0:T(8,128)(2,1)S(1)} %pad_maximum_fusion.2), channel_id=1, source_target_pairs={{0,32},{4,36},{8,40},{12,44},{16,48},{20,52},{24,56},{28,60},{32,0... | collective-permute-start | bytes 12296 | tf_op jit(solution)/shard_map/ppermute | solution.py:531
  84.2 16.0 %collective-permute-start.17 = (bf16[4,8,64]{2,1,0:T(8,128)(2,1)S(1)}, bf16[4,8,64]{2,1,0:T(8,128)(2,1)S(1)}, u32[]{:S(2)}, u32[]{:S(2)}) collective-permute-start(bf16[4,8,64]{2,1,0:T(8,128)(2,1)S(1)} %pad_maximum_fusion.2), channel_id=1, source_target_pairs={{0,48},{4,52},{8,56},{12,60},{16,32},{20,36},{24,40},{28,44},{32,1... | collective-permute-start | bytes 12296 | tf_op jit(solution)/shard_map/ppermute | solution.py:531
  100.2 22.0 %collective-permute-start.18 = (bf16[16,8,64]{2,1,0:T(8,128)(2,1)S(1)}, bf16[16,8,64]{2,1,0:T(8,128)(2,1)S(1)}, u32[]{:S(2)}, u32[]{:S(2)}) collective-permute-start(bf16[16,8,64]{2,1,0:T(8,128)(2,1)S(1)} %pad_maximum_fusion.1), channel_id=1, source_target_pairs={{0,64},{4,68},{8,72},{12,76},{16,80},{20,84},{24,88},{28,92},{32,9... | collective-permute-start | bytes 49160 | tf_op jit(solution)/shard_map/ppermute | solution.py:531
  103.8 18.5 %collective-permute-start.19 = (bf16[16,8,64]{2,1,0:T(8,128)(2,1)S(1)}, bf16[16,8,64]{2,1,0:T(8,128)(2,1)S(1)}, u32[]{:S(2)}, u32[]{:S(2)}) collective-permute-start(bf16[16,8,64]{2,1,0:T(8,128)(2,1)S(1)} %pad_maximum_fusion.1), channel_id=1, source_target_pairs={{0,128},{4,132},{8,136},{12,140},{16,144},{20,148},{24,152},{28,15... | collective-permute-start | bytes 49160 | tf_op jit(solution)/shard_map/ppermute | solution.py:531
  109.7 12.6 %collective-permute-start.20 = (bf16[16,8,64]{2,1,0:T(8,128)(2,1)S(1)}, bf16[16,8,64]{2,1,0:T(8,128)(2,1)S(1)}, u32[]{:S(2)}, u32[]{:S(2)}) collective-permute-start(bf16[16,8,64]{2,1,0:T(8,128)(2,1)S(1)} %pad_maximum_fusion.1), channel_id=1, source_target_pairs={{0,192},{4,196},{8,200},{12,204},{16,208},{20,212},{24,216},{28,22... | collective-permute-start | bytes 49160 | tf_op jit(solution)/shard_map/ppermute | solution.py:531
  (4 other events, 46.8 us)

commit v2 on v1

--- a/solution.py
+++ b/solution.py
@@ -16,7 +16,11 @@
 CLASSES = (128, 96, 64)
 COSTS = (5, 4, 3)
 OWN_UNITS = 2
-VMEM_LIMIT = 36 << 20
+VMEM_LIMIT = 33 << 20
+
+
+LEAF = "leaf"
+GATHER_ROWS = 16
 
 
 def shift(x, axis, by):
@@ -24,7 +28,8 @@
     return lax.ppermute(x, axis, [(i, (i + by) % count) for i in range(count)])
 
 
-def slide(x, axis, by):
+def slide(x, by):
+    axis = LEAF
     count = lax.axis_size(axis)
     pairs = [(i, i + by) for i in range(count) if 0 <= i + by < count]
     return lax.ppermute(x, axis, pairs)
@@ -360,13 +365,20 @@
     fan = leaves // boxes
 
     def body(w, _):
+        first = w * 2 * fan
+        moments = [
+            lax.dot_general(
+                local[w * 2 + j // fan], t1[first + j], across, preferred_element_type=jnp.float32
+            ).astype(bf)
+            for j in range(2 * fan)
+        ]
+        fars = [
+            jnp.dot(moments[j], basis[first + j], preferred_element_type=jnp.float32)
+            for j in range(2 * fan)
+        ]
         for j in range(2 * fan):
-            t = w * 2 * fan + j
-            moment = lax.dot_general(
-                local[w * 2 + j // fan], t1[t], across, preferred_element_type=jnp.float32
-            ).astype(bf)
-            far = jnp.dot(moment, basis[t], preferred_element_type=jnp.float32)
-            out_ref[t] = jnp.where(point < counts[t], near[t] + far, 0.0)
+            t = first + j
+            out_ref[t] = jnp.where(point < counts[t], near[t] + fars[j], 0.0)
         return 0
 
     lax.fori_loop(0, boxes // 2, body, 0)
@@ -462,8 +474,7 @@
     coupling3,
 ):
     lane = lax.axis_index("sub")
-    group = lax.axis_index("leaf")
-    leaves = lax.axis_size("leaf")
+    group = lax.axis_index(LEAF)
     lanes = lax.axis_size("sub")
     leaf_dev, rhs_count, points = charges.shape
     rank_size = basis.shape[1]
@@ -476,8 +487,8 @@
 
     blocks = gather_ring(charges, "sub")
     planes = jnp.transpose(coords, (1, 0, 2))
-    left_c = slide(planes, "leaf", 1)
-    right_c = slide(planes, "leaf", -1)
+    left_c = slide(planes, 1)
+    right_c = slide(planes, -1)
     own_counts = lax.dynamic_slice_in_dim(counts, start, leaf_dev, 0)
 
     slot = jnp.arange(group_size, dtype=jnp.int32)
@@ -488,8 +499,8 @@
     blocks, plan_own, plan_all = tie((blocks, plan_own, plan_all))
     mine = arrange(place, counts, blocks)
     mine, left_c, right_c = tie((mine, left_c, right_c))
-    left_q = slide(mine, "leaf", 1)
-    right_q = slide(mine, "leaf", -1)
+    left_q = slide(mine, 1)
+    right_q = slide(mine, -1)
 
     own_charges = lax.dynamic_slice_in_dim(mine, start, leaf_dev, 0)
     transfer_boxed = transfer1.reshape(clusters, 8, rank_size, rank_size)
@@ -503,47 +514,30 @@
         preferred_element_type=jnp.float32,
     ).astype(jnp.bfloat16)
 
-    rounds = (leaves.bit_length() - 1) // 2
-
-    def share_of(k):
-        return jnp.stack([jnp.int32(k), jnp.int32(k + 1), jnp.int32(rounds), start])
-
-    mine_after, box_moments = tie((mine, box_moments))
+    def share_of(low, high, parts):
+        return jnp.stack([jnp.int32(low), jnp.int32(high), jnp.int32(parts), start])
+
     ring = gather_ring(box_moments, "sub")
-    acc = near_own(share_of(0), plan_own, planes, mine_after, leaf_dev)
-    ring, acc = tie((ring, acc))
     group_moments = jnp.roll(jnp.stack(ring), lane, axis=0)
     group_moments = group_moments.reshape(group_boxes, rhs_count, rank_size)
     top_moment = jnp.einsum(
         "brc,bcp->rp", group_moments, transfer2, preferred_element_type=jnp.float32
     ).astype(jnp.bfloat16)
-
+    fill = ((0, GATHER_ROWS - 1), (0, 0), (0, 0))
+    top_moment, mine_after = tie((jnp.pad(top_moment[None], fill), mine))
+    table = lax.all_gather(top_moment, LEAF, axis=0, tiled=True)
+    acc = near_own(share_of(0, 1, 1), plan_own, planes, mine_after, leaf_dev)
+    group_moments, acc = tie((group_moments, acc))
+    left_b = slide(group_moments, 1)
+    right_b = slide(group_moments, -1)
+    acc, src_c, src_q = near_first(
+        share_of(0, 1, 1), plan_all, (left_c, planes, right_c), (left_q, mine, right_q), acc
+    )
     far2_local = jnp.clip(far2_list - (group - 1) * group_boxes, 0, 3 * group_boxes - 1)
     picks = jnp.where(far2_list >= 0, far2_local, 3 * group_boxes).reshape(-1)
-    table = top_moment[None]
-    box_far = None
-    for k in range(rounds):
-        if k == rounds - 1:
-            table, acc, box_far = tie((table, acc, box_far))
-        else:
-            table, acc = tie((table, acc))
-        others = [
-            lax.ppermute(table, "leaf", [(i, i ^ (m << 2 * k)) for i in range(leaves)])
-            for m in (1, 2, 3)
-        ]
-        if k == 0:
-            left_b = slide(group_moments, "leaf", 1)
-            right_b = slide(group_moments, "leaf", -1)
-            acc, src_c, src_q = near_first(
-                share_of(k), plan_all, (left_c, planes, right_c), (left_q, mine, right_q), acc
-            )
-            others, left_b, right_b, acc = tie((others, left_b, right_b, acc))
-        else:
-            acc = near_next(share_of(k), plan_all, src_c, src_q, acc)
-        if k == 1:
-            box_far = box_field(picks, left_b, group_moments, right_b, coupling2)
-        table = jnp.concatenate([table] + list(others), axis=0)
-    flips = jnp.where(far3_list[0] >= 0, far3_list[0] ^ group, -1)
+    left_b, acc = tie((left_b, acc))
+    box_far = box_field(picks, left_b, group_moments, right_b, coupling2)
+    flips = jnp.where(far3_list[0] >= 0, far3_list[0] * GATHER_ROWS, -1)
     lane_box = (lane * clusters)[None]
     return go_down(
         flips,
@@ -564,19 +558,19 @@
         on_device,
         mesh=mesh,
         in_specs=(
-            P("leaf", None, None),
-            P(("leaf", "sub"), None, None),
-            P("leaf"),
-            P("leaf"),
-            P(("leaf", "sub"), None),
-            P(("leaf", "sub"), None, None),
-            P(("leaf", "sub"), None, None),
-            P(("leaf", "sub"), None),
-            P(("leaf", "sub"), None, None, None),
-            P("leaf", None, None),
-            P("leaf", None),
-            P("leaf", None, None, None),
-        ),
-        out_specs=P(("leaf", "sub"), None, None),
+            P(LEAF, None, None),
+            P((LEAF, "sub"), None, None),
+            P(LEAF),
+            P(LEAF),
+            P((LEAF, "sub"), None),
+            P((LEAF, "sub"), None, None),
+            P((LEAF, "sub"), None, None),
+            P((LEAF, "sub"), None),
+            P((LEAF, "sub"), None, None, None),
+            P(LEAF, None, None),
+            P(LEAF, None),
+            P(LEAF, None, None, None),
+        ),
+        out_specs=P((LEAF, "sub"), None, None),
         check_vma=False,
     )

time: 144 us -> 143 us (level)
  starting transfers between devices: 49.8 us -> 26 us
  between operations: 0.48 us -> 13.8 us
  local copies, waits for them, and re-layouts: 5.56 us -> 18.5 us
  Pallas kernels: 76.6 us -> 64.7 us
  waiting for transfers between devices: 0.06 us -> 10.5 us
  other arithmetic: 7.43 us -> 5.87 us
    pallas_call x1, Pallas kernels: 12.3 us -> 38.9 us  [near_first(): pl.pallas_call(near_first_kernel, out_shape=(jax.ShapeDtypeStruct(acc.sha...]
    pallas_call x2 -> x0, Pallas kernels: 24.1 us -> none  [near_next(): pl.pallas_call(near_next_kernel, out_shape=jax.ShapeDtypeStruct(acc.shape...]
    ppermute x9 -> x0, starting transfers between devices: 23.4 us -> none  [on_device(): lax.ppermute(table, 'leaf', [(i, i ^ m << 2 * k) for i in range(leaves)])]
    pallas_call x1, Pallas kernels: 19.5 us -> 4.73 us  [go_down(): pl.pallas_call(down_kernel, out_shape=jax.ShapeDtypeStruct((leaves,) + ne...]
    unnamed x23 -> x42, local copies, waits for them, and re-layouts: 4.13 us -> 15 us
    all_gather x0 -> x1, waiting for transfers between devices: none -> 7.72 us  [on_device(): table = lax.all_gather(top_moment, LEAF, axis=0, tiled=True)]
    ppermute x6, waiting for transfers between devices: 0.02 us -> 2.74 us  [shift(): return lax.ppermute(x, axis, [(i, (i + by) % count) for i in range(count)])]
  transfers between devices with their start and end apart: 21 -> 13, of which waited for: 0 -> 3; matrix products, arithmetic and copies ran while one was open for 9% -> 9% of each run, Pallas kernels for 40% -> 42%
where the time goes in v2:
time: 143 us; the launch traced here: 142 us
  Pallas kernels  64.7 us (45%)
  starting transfers between devices  26 us (18%)
  local copies, waits for them, and re-layouts  18.5 us (13%)
  between operations  13.8 us (10%)
  waiting for transfers between devices  10.5 us (7%)
  other arithmetic  5.87 us (4%)
  matrix products  2.55 us (2%)
    pallas_call x1, Pallas kernels, near_first(): pl.pallas_call(near_first_kernel, out_shape=(jax.ShapeDtypeStruct(acc.sha...  38.9 us
    ppermute x6, starting transfers between devices, slide(): return lax.ppermute(x, axis, pairs)  18 us
    pallas_call x1, Pallas kernels, near_own(): pl.pallas_call(near_own_kernel, out_shape=jax.ShapeDtypeStruct((targets +...  17.7 us
    unnamed x42, local copies, waits for them, and re-layouts  15 us
    ppermute x6, starting transfers between devices, shift(): return lax.ppermute(x, axis, [(i, (i + by) % count) for i in range(count)])  8 us
    all_gather x1, waiting for transfers between devices, on_device(): table = lax.all_gather(top_moment, LEAF, axis=0, tiled=True)  7.72 us
    pallas_call x1, Pallas kernels, go_down(): pl.pallas_call(down_kernel, out_shape=jax.ShapeDtypeStruct((leaves,) + ne...  4.73 us
  transfers between devices with their start and end apart: 13, of which 3 were waited for; matrix products, arithmetic and copies ran while one was open for 9% of the time, Pallas kernels for 42%

profile of v2, /device:TPU:1, one launch (start us, length us, event | category | flops | bytes accessed | tf_op | source)
XLA Modules:
  0.0 141.9 jit_solution(3603908208300548315)
XLA Ops:
  6.5 3.6 %collective-permute-start = (bf16[128,8,128]{2,1,0:T(8,128)(2,1)}, bf16[128,8,128]{2,1,0:T(8,128)(2,1)S(1)}, u32[]{:S(2)}, u32[]{:S(2)}) collective-permute-start(bf16[128,8,128]{2,1,0:T(8,128)(2,1)} %b0), channel_id=1, source_target_pairs={{0,3},{1,0},{2,1},{3,2},{4,7},{5,4},{6,5},{7,6},{8,11},{9,8},{10,9... | collective-permute-start | bytes 786440 | tf_op jit(solution)/shard_map/ppermute | solution.py:28
  11.1 4.5 %collective-permute-start.3 = (bf16[3,512,128]{2,1,0:T(8,128)(2,1)}, bf16[3,512,128]{2,1,0:T(8,128)(2,1)}, u32[]{:S(2)}, u32[]{:S(2)}) collective-permute-start(bf16[3,512,128]{2,1,0:T(8,128)(2,1)} %bitcast.47), channel_id=1, source_target_pairs={{0,4},{4,8},{8,12},{12,16},{16,20},{20,24},{24,28},{28,32},{32,36}... | collective-permute-start | bytes 1179656 | tf_op jit(solution)/shard_map/ppermute | solution.py:35
  15.7 1.9 %collective-permute-start.4 = (bf16[3,512,128]{2,1,0:T(8,128)(2,1)}, bf16[3,512,128]{2,1,0:T(8,128)(2,1)}, u32[]{:S(2)}, u32[]{:S(2)}) collective-permute-start(bf16[3,512,128]{2,1,0:T(8,128)(2,1)} %bitcast.48), channel_id=1, source_target_pairs={{4,0},{8,4},{12,8},{16,12},{20,16},{24,20},{28,24},{32,28},{36,32}... | collective-permute-start | bytes 1179656 | tf_op jit(solution)/shard_map/ppermute | solution.py:35
  24.8 3.9 %copy.32.t1 = bf16[128,64,64]{2,1,0:T(8,128)(2,1)S(1)} copy(bf16[128,64,64]{0,2,1:T(8,128)(2,1)} %param.18) | data formatting | bytes 2097152 | tf_op args[6]
  28.8 1.6 %arrange.1.q_ref.q1 = bf16[512,8,128]{2,1,0:T(8,128)(2,1)S(1)} custom-call(s32[512]{0:T(512)S(1)} %fusion.16.place, s32[512]{0:T(512)S(1)} %copy-done.12, bf16[128,8,128]{2,1,0:T(8,128)(2,1)S(1)} %copy-done.10, bf16[128,8,128]{2,1,0:T(8,128)(2,1)S(1)} %collective-permute-done.b1, bf16[128,8,128]{2,1,0:T(8,128)(2,1)S(1)} %collective-permute-done.1.b2, ...), custom_call_target="tpu_custom_call" | custom-call | flops 1048576 | bytes 2097152 | tf_op jit(solution)/shard_map/arrange/pallas_call | solution.py:91
  30.5 1.2 convolution_convert_fusion
  31.7 1.1 bitcast_dynamic-update-slice_fusion.6
  32.7 2.0 %collective-permute-start.5 = (bf16[16,8,64]{2,1,0:T(8,128)(2,1)S(1)}, bf16[16,8,64]{2,1,0:T(8,128)(2,1)S(1)}, u32[]{:S(2)}, u32[]{:S(2)}) collective-permute-start(bf16[16,8,64]{2,1,0:T(8,128)(2,1)S(1)} %get-tuple-element.71), channel_id=1, source_target_pairs={{0,3},{1,0},{2,1},{3,2},{4,7},{5,4},{6,5},{7,6},{8,11},{9,8},{10,9... | collective-permute-start | bytes 49160 | tf_op jit(solution)/shard_map/ppermute | solution.py:28
  34.7 1.4 collective-permute-start.6
  36.8 2.2 %collective-permute-done.6 = bf16[16,8,64]{2,1,0:T(8,128)(2,1)S(1)} collective-permute-done((bf16[16,8,64]{2,1,0:T(8,128)(2,1)S(1)}, bf16[16,8,64]{2,1,0:T(8,128)(2,1)S(1)}, u32[]{:S(2)}, u32[]{:S(2)}) %collective-permute-start.6) | collective-permute-done | bytes 16416 | tf_op jit(solution)/shard_map/ppermute | solution.py:28
  45.1 2.0 %collective-permute-start.10 = (bf16[512,8,128]{2,1,0:T(8,128)(2,1)}, bf16[512,8,128]{2,1,0:T(8,128)(2,1)}, u32[]{:S(2)}, u32[]{:S(2)}) collective-permute-start(bf16[512,8,128]{2,1,0:T(8,128)(2,1)} %copy-done.5), channel_id=1, source_target_pairs={{4,0},{8,4},{12,8},{16,12},{20,16},{24,20},{28,24},{32,28},{36,32}... | collective-permute-start | bytes 3145736 | tf_op jit(solution)/shard_map/ppermute | solution.py:35
  47.1 5.2 %collective-permute-start.9 = (bf16[512,8,128]{2,1,0:T(8,128)(2,1)}, bf16[512,8,128]{2,1,0:T(8,128)(2,1)}, u32[]{:S(2)}, u32[]{:S(2)}) collective-permute-start(bf16[512,8,128]{2,1,0:T(8,128)(2,1)} %copy-done.5), channel_id=1, source_target_pairs={{0,4},{4,8},{8,12},{12,16},{16,20},{20,24},{24,28},{28,32},{32,36}... | collective-permute-start | bytes 3145736 | tf_op jit(solution)/shard_map/ppermute | solution.py:35
  52.6 1.2 copy-done.6
  53.8 1.0 copy-done.13
  54.8 17.7 %near_own.1.acc_in = f32[129,8,128]{2,1,0:T(8,128)S(1)} custom-call(s32[4]{0:T(128)S(1)} %pad_add_fusion.2.share, s32[912]{0:T(1024)S(1)} %get-tuple-element.35.w, s32[4128]{0:T(1024)S(1)} %compare_select_fusion.l, s32[5]{0:T(128)S(1)} %fusion.19.b, s32[129]{0:T(256)S(1)} %pad.13.r, s32[128]{0:T(128)S(1)} %select_reduce_fusion.5.o, ...), custom_call_target="tpu_custom_call" | custom-call | flops 4294967296 | bytes 1048576 | tf_op jit(solution)/shard_map/near_own/pallas_call | solution.py:241
  72.5 1.9 %collective-permute-start.8 = (bf16[64,8,64]{2,1,0:T(8,128)(2,1)S(1)}, bf16[64,8,64]{2,1,0:T(8,128)(2,1)S(1)}, u32[]{:S(2)}, u32[]{:S(2)}) collective-permute-start(bf16[64,8,64]{2,1,0:T(8,128)(2,1)S(1)} %bitcast.43), channel_id=1, source_target_pairs={{0,4},{4,8},{8,12},{12,16},{16,20},{20,24},{24,28},{28,32},{32,36}... | collective-permute-start | bytes 196616 | tf_op jit(solution)/shard_map/ppermute | solution.py:35
  74.5 2.4 %collective-permute-start.11 = (bf16[64,8,64]{2,1,0:T(8,128)(2,1)S(1)}, bf16[64,8,64]{2,1,0:T(8,128)(2,1)S(1)}, u32[]{:S(2)}, u32[]{:S(2)}) collective-permute-start(bf16[64,8,64]{2,1,0:T(8,128)(2,1)S(1)} %bitcast.44), channel_id=1, source_target_pairs={{4,0},{8,4},{12,8},{16,12},{20,16},{24,20},{28,24},{32,28},{36,32}... | collective-permute-start | bytes 196616 | tf_op jit(solution)/shard_map/ppermute | solution.py:35
  76.9 38.9 %near_first.1 = (f32[129,8,128]{2,1,0:T(8,128)S(1)}, f32[3,1544,128]{2,1,0:T(8,128)}, bf16[1537,8,128]{2,1,0:T(8,128)(2,1)}) custom-call(s32[4]{0:T(128)S(1)} %pad_add_fusion.2.share, s32[912]{0:T(1024)S(1)} %get-tuple-element.42.w, s32[4128]{0:T(1024)S(1)} %reshape.92.l, s32[5]{0:T(128)S(1)} %fusion.20.b, s32[129]{0:T(256)S(1)} %pad.13.r, ...), custom_call_target="tpu_custom_call" | custom-call | flops 4294967296 | bytes 1048576 | tf_op jit(solution)/shard_map/near_first/pallas_call | solution.py:264
  116.6 1.7 %box_field.1.box_far = f32[16,8,64]{2,1,0:T(8,128)S(1)} custom-call(s32[256]{0:T(256)S(1)} %reshape.96.picks, bf16[64,8,64]{2,1,0:T(8,128)(2,1)S(1)} %collective-permute-done.8.left, bf16[64,8,64]{2,1,0:T(8,128)(2,1)S(1)} %bitcast.45, bf16[64,8,64]{2,1,0:T(8,128)(2,1)S(1)} %collective-permute-done.11.right, bf16[256,64,64]{2,1,0:T(8,128)(2,1)S(1)} %bitcast.41), custom_call_target="tpu_custom_call" | custom-call | flops 16777216 | bytes 4194304 | tf_op jit(solution)/shard_map/box_field/pallas_call | solution.py:333
  118.4 7.7 %all-gather.2.cloned.1.call-done.table = bf16[1024,8,64]{2,1,0:T(8,128)(2,1)} async-done(((bf16[16,8,64]{2,1,0:T(8,128)(2,1)}), bf16[1024,8,64]{2,1,0:T(8,128)(2,1)}) %all-gather.2.cloned.1.call-update) | async-done | bytes 1048592 | tf_op jit(solution)/shard_map/all_gather | solution.py:528
  126.1 1.6 %copy-done.1 = bf16[128,64,128]{2,1,0:T(8,128)(2,1)S(1)} copy-done((bf16[128,64,128]{2,1,0:T(8,128)(2,1)S(1)}, bf16[128,64,128]{2,1,0:T(8,128)(2,1)}, u32[]{:S(2)}) %copy-start.1) | copy-done | bytes 2097176
  127.7 1.6 %copy-done.4 = bf16[1024,8,64]{2,1,0:T(8,128)(2,1)S(1)} copy-done((bf16[1024,8,64]{2,1,0:T(8,128)(2,1)S(1)}, bf16[1024,8,64]{2,1,0:T(8,128)(2,1)}, u32[]{:S(2)}) %copy-start.4) | copy-done | bytes 1048600
  129.3 1.0 copy-done.9
  130.3 4.7 %go_down.1 = f32[128,8,128]{2,1,0:T(8,128)} custom-call(s32[8]{0:T(128)S(1)} %fusion.21.flips, s32[128]{0:T(128)S(1)} %get-tuple-element.65.counts, s32[1]{0:T(128)} %bitcast.1.share, bf16[1024,8,64]{2,1,0:T(8,128)(2,1)S(1)} %copy-done.4, bf16[8,64,64]{2,1,0:T(8,128)(2,1)S(1)} %bitcast.46, bf16[64,64,64]{2,1,0:T(8,128)(2,1)S(1)} %copy-done.2, ...), custom_call_target="tpu_custom_call" | custom-call | flops 67108864 | bytes 5242880 | tf_op jit(solution)/shard_map/go_down/pallas_call | solution.py:389
  (88 shorter events, 15.9 us)
Async XLA Ops:
  6.5 22.3 %copy-start.10 = (bf16[128,8,128]{2,1,0:T(8,128)(2,1)S(1)}, bf16[128,8,128]{2,1,0:T(8,128)(2,1)}, u32[]{:S(2)}) copy-start(bf16[128,8,128]{2,1,0:T(8,128)(2,1)} %b0) | copy-start | bytes 786436
  6.5 22.3 %copy-start.12 = (s32[512]{0:T(512)S(1)}, s32[512]{0:T(512)}, u32[]{:S(2)}) copy-start(s32[512]{0:T(512)} %counts.1) | copy-start | bytes 6148
  6.5 119.6 %all-gather.2.cloned.1.call-start = ((), (), s32[]{:S(2)}) async-start(), calls=%async_computation | async-start | bytes 2129920 | tf_op jit(solution)/shard_map/all_gather | solution.py:528
  6.5 22.2 %collective-permute-start = (bf16[128,8,128]{2,1,0:T(8,128)(2,1)}, bf16[128,8,128]{2,1,0:T(8,128)(2,1)S(1)}, u32[]{:S(2)}, u32[]{:S(2)}) collective-permute-start(bf16[128,8,128]{2,1,0:T(8,128)(2,1)} %b0), channel_id=1, source_target_pairs={{0,3},{1,0},{2,1},{3,2},{4,7},{5,4},{6,5},{7,6},{8,11},{9,8},{10,9... | collective-permute-start | bytes 786440 | tf_op jit(solution)/shard_map/ppermute | solution.py:28
  10.1 18.7 %collective-permute-start.1 = (bf16[128,8,128]{2,1,0:T(8,128)(2,1)}, bf16[128,8,128]{2,1,0:T(8,128)(2,1)S(1)}, u32[]{:S(2)}, u32[]{:S(2)}) collective-permute-start(bf16[128,8,128]{2,1,0:T(8,128)(2,1)} %b0), channel_id=1, source_target_pairs={{0,2},{1,3},{2,0},{3,1},{4,6},{5,7},{6,4},{7,5},{8,10},{9,11},{10,... | collective-permute-start | bytes 786440 | tf_op jit(solution)/shard_map/ppermute | solution.py:28
  10.5 18.4 %collective-permute-start.2 = (bf16[128,8,128]{2,1,0:T(8,128)(2,1)}, bf16[128,8,128]{2,1,0:T(8,128)(2,1)S(1)}, u32[]{:S(2)}, u32[]{:S(2)}) collective-permute-start(bf16[128,8,128]{2,1,0:T(8,128)(2,1)} %b0), channel_id=1, source_target_pairs={{0,1},{1,2},{2,3},{3,0},{4,5},{5,6},{6,7},{7,4},{8,9},{9,10},{10,1... | collective-permute-start | bytes 786440 | tf_op jit(solution)/shard_map/ppermute | solution.py:28
  11.1 19.3 %collective-permute-start.3 = (bf16[3,512,128]{2,1,0:T(8,128)(2,1)}, bf16[3,512,128]{2,1,0:T(8,128)(2,1)}, u32[]{:S(2)}, u32[]{:S(2)}) collective-permute-start(bf16[3,512,128]{2,1,0:T(8,128)(2,1)} %bitcast.47), channel_id=1, source_target_pairs={{0,4},{4,8},{8,12},{12,16},{16,20},{20,24},{24,28},{28,32},{32,36}... | collective-permute-start | bytes 1179656 | tf_op jit(solution)/shard_map/ppermute | solution.py:35
  15.7 14.8 %collective-permute-start.4 = (bf16[3,512,128]{2,1,0:T(8,128)(2,1)}, bf16[3,512,128]{2,1,0:T(8,128)(2,1)}, u32[]{:S(2)}, u32[]{:S(2)}) collective-permute-start(bf16[3,512,128]{2,1,0:T(8,128)(2,1)} %bitcast.48), channel_id=1, source_target_pairs={{4,0},{8,4},{12,8},{16,12},{20,16},{24,20},{28,24},{32,28},{36,32}... | collective-permute-start | bytes 1179656 | tf_op jit(solution)/shard_map/ppermute | solution.py:35
  28.8 1.7 %copy-start = (bf16[128,64,128]{2,1,0:T(8,128)(2,1)S(1)}, bf16[128,64,128]{2,1,0:T(8,128)(2,1)}, u32[]{:S(2)}) copy-start(bf16[128,64,128]{2,1,0:T(8,128)(2,1)} %basis.1) | copy-start | bytes 6291460
  30.4 2.3 %copy-start.5 = (bf16[512,8,128]{2,1,0:T(8,128)(2,1)}, bf16[512,8,128]{2,1,0:T(8,128)(2,1)S(1)}, u32[]{:S(2)}) copy-start(bf16[512,8,128]{2,1,0:T(8,128)(2,1)S(1)} %arrange.1.q_ref.q1) | copy-start | bytes 3145732
  31.7 12.5 %copy-start.2 = (bf16[64,64,64]{2,1,0:T(8,128)(2,1)S(1)}, bf16[64,64,64]{2,1,0:T(8,128)(2,1)}, u32[]{:S(2)}) copy-start(bf16[64,64,64]{2,1,0:T(8,128)(2,1)} %t2.1) | copy-start | bytes 1572868
  31.7 20.7 %copy-start.15 = (s32[16,16]{1,0:T(8,128)S(1)}, s32[16,16]{1,0:T(8,128)}, u32[]{:S(2)}) copy-start(s32[16,16]{1,0:T(8,128)} %param.19) | copy-start | bytes 3076
  31.7 20.9 %copy-start.16 = (s32[1,8]{1,0:T(1,128)S(1)}, s32[1,8]{1,0:T(1,128)}, u32[]{:S(2)}) copy-start(s32[1,8]{1,0:T(1,128)} %param.22) | copy-start | bytes 100
  32.7 3.4 %collective-permute-start.5 = (bf16[16,8,64]{2,1,0:T(8,128)(2,1)S(1)}, bf16[16,8,64]{2,1,0:T(8,128)(2,1)S(1)}, u32[]{:S(2)}, u32[]{:S(2)}) collective-permute-start(bf16[16,8,64]{2,1,0:T(8,128)(2,1)S(1)} %get-tuple-element.71), channel_id=1, source_target_pairs={{0,3},{1,0},{2,1},{3,2},{4,7},{5,4},{6,5},{7,6},{8,11},{9,8},{10,9... | collective-permute-start | bytes 49160 | tf_op jit(solution)/shard_map/ppermute | solution.py:28
  34.7 4.3 %collective-permute-start.6 = (bf16[16,8,64]{2,1,0:T(8,128)(2,1)S(1)}, bf16[16,8,64]{2,1,0:T(8,128)(2,1)S(1)}, u32[]{:S(2)}, u32[]{:S(2)}) collective-permute-start(bf16[16,8,64]{2,1,0:T(8,128)(2,1)S(1)} %get-tuple-element.71), channel_id=1, source_target_pairs={{0,2},{1,3},{2,0},{3,1},{4,6},{5,7},{6,4},{7,5},{8,10},{9,11},{10,... | collective-permute-start | bytes 49160 | tf_op jit(solution)/shard_map/ppermute | solution.py:28
  36.1 4.0 %collective-permute-start.7 = (bf16[16,8,64]{2,1,0:T(8,128)(2,1)S(1)}, bf16[16,8,64]{2,1,0:T(8,128)(2,1)S(1)}, u32[]{:S(2)}, u32[]{:S(2)}) collective-permute-start(bf16[16,8,64]{2,1,0:T(8,128)(2,1)S(1)} %get-tuple-element.71), channel_id=1, source_target_pairs={{0,1},{1,2},{2,3},{3,0},{4,5},{5,6},{6,7},{7,4},{8,9},{9,10},{10,1... | collective-permute-start | bytes 49160 | tf_op jit(solution)/shard_map/ppermute | solution.py:28
  45.1 31.8 %collective-permute-start.10 = (bf16[512,8,128]{2,1,0:T(8,128)(2,1)}, bf16[512,8,128]{2,1,0:T(8,128)(2,1)}, u32[]{:S(2)}, u32[]{:S(2)}) collective-permute-start(bf16[512,8,128]{2,1,0:T(8,128)(2,1)} %copy-done.5), channel_id=1, source_target_pairs={{4,0},{8,4},{12,8},{16,12},{20,16},{24,20},{28,24},{32,28},{36,32}... | collective-permute-start | bytes 3145736 | tf_op jit(solution)/shard_map/ppermute | solution.py:35
  47.1 29.8 %collective-permute-start.9 = (bf16[512,8,128]{2,1,0:T(8,128)(2,1)}, bf16[512,8,128]{2,1,0:T(8,128)(2,1)}, u32[]{:S(2)}, u32[]{:S(2)}) collective-permute-start(bf16[512,8,128]{2,1,0:T(8,128)(2,1)} %copy-done.5), channel_id=1, source_target_pairs={{0,4},{4,8},{8,12},{12,16},{16,20},{20,24},{24,28},{28,32},{32,36}... | collective-permute-start | bytes 3145736 | tf_op jit(solution)/shard_map/ppermute | solution.py:35
  54.8 22.1 %copy-start.7 = (bf16[512,8,128]{2,1,0:T(8,128)(2,1)S(1)}, bf16[512,8,128]{2,1,0:T(8,128)(2,1)}, u32[]{:S(2)}) copy-start(bf16[512,8,128]{2,1,0:T(8,128)(2,1)} %copy-done.5) | copy-start | bytes 3145732
  54.8 22.1 %copy-start.14 = (bf16[512,3,128]{2,0,1:T(8,128)(2,1)S(1)}, bf16[512,3,128]{2,0,1:T(8,128)(2,1)}, u32[]{:S(2)}) copy-start(bf16[512,3,128]{2,0,1:T(8,128)(2,1)} %param.12) | copy-start | bytes 1179652
  72.5 44.1 %collective-permute-start.8 = (bf16[64,8,64]{2,1,0:T(8,128)(2,1)S(1)}, bf16[64,8,64]{2,1,0:T(8,128)(2,1)S(1)}, u32[]{:S(2)}, u32[]{:S(2)}) collective-permute-start(bf16[64,8,64]{2,1,0:T(8,128)(2,1)S(1)} %bitcast.43), channel_id=1, source_target_pairs={{0,4},{4,8},{8,12},{12,16},{16,20},{20,24},{24,28},{28,32},{32,36}... | collective-permute-start | bytes 196616 | tf_op jit(solution)/shard_map/ppermute | solution.py:35
  74.5 42.2 %collective-permute-start.11 = (bf16[64,8,64]{2,1,0:T(8,128)(2,1)S(1)}, bf16[64,8,64]{2,1,0:T(8,128)(2,1)S(1)}, u32[]{:S(2)}, u32[]{:S(2)}) collective-permute-start(bf16[64,8,64]{2,1,0:T(8,128)(2,1)S(1)} %bitcast.44), channel_id=1, source_target_pairs={{4,0},{8,4},{12,8},{16,12},{20,16},{24,20},{28,24},{32,28},{36,32}... | collective-permute-start | bytes 196616 | tf_op jit(solution)/shard_map/ppermute | solution.py:35
  76.9 39.7 %copy-start.3 = (bf16[16,16,64,64]{3,2,1,0:T(8,128)(2,1)S(1)}, bf16[16,16,64,64]{3,2,1,0:T(8,128)(2,1)}, u32[]{:S(2)}) copy-start(bf16[16,16,64,64]{3,2,1,0:T(8,128)(2,1)} %param.20) | copy-start | bytes 6291460
  116.6 9.5 %copy-start.11 = (bf16[1,8,64,64]{3,2,1,0:T(8,128)(2,1)S(1)}, bf16[1,8,64,64]{3,2,1,0:T(8,128)(2,1)}, u32[]{:S(2)}) copy-start(bf16[1,8,64,64]{3,2,1,0:T(8,128)(2,1)} %param.23) | copy-start | bytes 196612
  (6 other events, 7.2 us)
Sparse Core Ops, SparseCore 0:
  45.2 80.8 all-gather.1

commit v3 on v1

--- a/solution.py
+++ b/solution.py
@@ -17,6 +17,9 @@
 COSTS = (5, 4, 3)
 OWN_UNITS = 2
 VMEM_LIMIT = 36 << 20
+
+in_vmem = pl.BlockSpec(memory_space=pltpu.VMEM)
+in_place = pl.BlockSpec(memory_space=pl.ANY)
 
 
 def shift(x, axis, by):
@@ -58,8 +61,9 @@
         tile_t[targets * 3 + c] = jnp.zeros((128, 128), jnp.float32)
 
 
-def arrange_kernel(place, counts, b0, b1, b2, b3, out_ref, held, sems):
+def arrange_kernel(place, counts, b0, b1, b2, b3, coords, out_ref, held, sems):
     rows = b0.shape[0]
+    leaves = place.shape[0]
     copies = [
         pltpu.make_async_copy(b, held.at[pl.ds(k * rows, rows)], sems.at[k])
         for k, b in enumerate((b0, b1, b2, b3))
@@ -77,20 +81,22 @@
             out_ref[s] = jnp.where(point < counts[s], row, 0.0).astype(jnp.bfloat16)
         return 0
 
-    lax.fori_loop(0, out_ref.shape[0] // 16, body, 0)
-
-
-def arrange(place, counts, blocks):
+    out_ref[leaves:] = coords[...]
+    lax.fori_loop(0, leaves // 16, body, 0)
+
+
+def arrange(place, counts, blocks, planes):
     leaves = place.shape[0]
+    coords = planes.reshape(-1, 8, 128)
     whole = pl.BlockSpec(memory_space=pl.ANY)
     return pl.pallas_call(
         arrange_kernel,
-        out_shape=jax.ShapeDtypeStruct((leaves, 8, 128), jnp.bfloat16),
+        out_shape=jax.ShapeDtypeStruct((leaves + coords.shape[0], 8, 128), jnp.bfloat16),
         grid_spec=pltpu.PrefetchScalarGridSpec(
             num_scalar_prefetch=2,
             grid=(),
-            in_specs=[whole] * 4,
-            out_specs=pl.BlockSpec(memory_space=pltpu.VMEM),
+            in_specs=[whole] * 4 + [in_vmem],
+            out_specs=in_vmem,
             scratch_shapes=[
                 pltpu.VMEM((leaves, 8, 128), jnp.bfloat16),
                 pltpu.SemaphoreType.DMA((4,)),
@@ -99,7 +105,7 @@
         compiler_params=pltpu.CompilerParams(vmem_limit_bytes=8 << 20),
         cost_estimate=pl.CostEstimate(flops=1 << 20, bytes_accessed=2 << 20, transcendentals=0),
         name="arrange",
-    )(place, counts, *blocks)
+    )(place, counts, *blocks, coords)
 
 
 def split(bounds, part, parts):
@@ -175,39 +181,53 @@
         lax.fori_loop(first, jnp.maximum(first, last), functools.partial(step, rows), 0)
 
 
-def spread_coords(planes, src_c):
-    group = planes[0].shape[1]
-    for c in range(3):
-        for k, plane in enumerate(planes):
-            src_c[c, k * group : (k + 1) * group, :] = plane[c].astype(jnp.float32)
-        src_c[c, len(planes) * group :, :] = jnp.zeros((8, 128), jnp.float32)
-
-
 def near_own_kernel(share, w, l, b, r, o, c_ref, q_ref, acc, tile_t, src_c, src_q, sem):
-    group = q_ref.shape[0]
-    copy = pltpu.make_async_copy(q_ref, src_q.at[pl.ds(0, group)], sem)
+    group = c_ref.shape[1]
+    copy = pltpu.make_async_copy(q_ref.at[pl.ds(0, group)], src_q.at[pl.ds(0, group)], sem)
     copy.start()
     src_q[group] = jnp.zeros(src_q.shape[1:], src_q.dtype)
-    spread_coords([c_ref], src_c)
+    for c in range(3):
+        src_c[c, :group, :] = c_ref[c].astype(jnp.float32)
+        src_c[c, group:, :] = jnp.zeros((8, 128), jnp.float32)
     acc[...] = jnp.zeros_like(acc)
     copy.wait()
     near_steps((w, l, b, r, o), 0, b[3], share[3], tile_t, src_c, src_q, acc, group)
 
 
 def near_first_kernel(
-    share, w, l, b, r, o, c0, c1, c2, q0, q1, q2, acc_in, acc, src_c, src_q, tile_t, sems
+    share, w, l, b, r, o, x0, x1, x2, acc_in, acc, src_c, src_q, tile_t, stage, sems
 ):
-    group = q0.shape[0]
+    packs = (x0, x1, x2)
+    eights = stage.shape[1]
+    group = x0.shape[0] - eights
     copies = [
-        pltpu.make_async_copy(q, src_q.at[pl.ds(k * group, group)], sems.at[k])
-        for k, q in enumerate((q0, q1, q2))
+        pltpu.make_async_copy(x.at[pl.ds(group, eights)], stage.at[k], sems.at[k, 0])
+        for k, x in enumerate(packs)
+    ] + [
+        pltpu.make_async_copy(
+            x.at[pl.ds(0, group)], src_q.at[pl.ds(k * group, group)], sems.at[k, 1]
+        )
+        for k, x in enumerate(packs)
     ]
     for copy in copies:
         copy.start()
     src_q[3 * group] = jnp.zeros(src_q.shape[1:], src_q.dtype)
-    spread_coords([c0, c1, c2], src_c)
     acc[...] = acc_in[...]
-    for copy in copies:
+    for copy in copies[:3]:
+        copy.wait()
+    for c in range(3):
+        src_c[c, 3 * group :, :] = jnp.zeros((8, 128), jnp.float32)
+
+        def spread(w, _):
+            for k in range(3):
+                for j in range(4):
+                    i = w * 4 + j
+                    rows = pl.ds(pl.multiple_of(k * group + 8 * i, 8), 8)
+                    src_c[c, rows, :] = stage[k, c * (group // 8) + i].astype(jnp.float32)
+            return 0
+
+        lax.fori_loop(0, group // 32, spread, 0)
+    for copy in copies[3:]:
         copy.wait()
     high = split(b, share[1], share[2])
     near_steps((w, l, b, r, o), 0, high, group + share[3], tile_t, src_c, src_q, acc, 0)
@@ -223,8 +243,6 @@
 
 near_params = pltpu.CompilerParams(vmem_limit_bytes=VMEM_LIMIT)
 near_cost = pl.CostEstimate(flops=1 << 32, bytes_accessed=1 << 20, transcendentals=50 << 20)
-in_vmem = pl.BlockSpec(memory_space=pltpu.VMEM)
-in_place = pl.BlockSpec(memory_space=pl.ANY)
 
 
 def tile_scratch(targets):
@@ -232,7 +250,7 @@
 
 
 def near_own(share, plan, coords, charges, targets):
-    group = charges.shape[0]
+    group = coords.shape[1]
     return pl.pallas_call(
         near_own_kernel,
         out_shape=jax.ShapeDtypeStruct((targets + 1, 8, 128), jnp.float32),
@@ -254,8 +272,7 @@
     )(share, *plan, coords, charges)
 
 
-def near_first(share, plan, coords, charges, acc):
-    group = charges[0].shape[0]
+def near_first(share, plan, packs, acc, group):
     return pl.pallas_call(
         near_first_kernel,
         out_shape=(
@@ -266,14 +283,18 @@
         grid_spec=pltpu.PrefetchScalarGridSpec(
             num_scalar_prefetch=6,
             grid=(),
-            in_specs=[in_vmem] * 3 + [in_place] * 3 + [in_vmem],
+            in_specs=[in_place] * 3 + [in_vmem],
             out_specs=(in_vmem,) * 3,
-            scratch_shapes=[tile_scratch(acc.shape[0] - 1), pltpu.SemaphoreType.DMA((3,))],
+            scratch_shapes=[
+                tile_scratch(acc.shape[0] - 1),
+                pltpu.VMEM((3, packs[0].shape[0] - group, 8, 128), jnp.bfloat16),
+                pltpu.SemaphoreType.DMA((3, 2)),
+            ],
         ),
         compiler_params=near_params,
         cost_estimate=near_cost,
         name="near_first",
-    )(share, *plan, *coords, *charges, acc)
+    )(share, *plan, *packs, acc)
 
 
 def near_next(share, plan, src_c, src_q, acc):
@@ -360,13 +381,20 @@
     fan = leaves // boxes
 
     def body(w, _):
+        first = w * 2 * fan
+        moments = [
+            lax.dot_general(
+                local[w * 2 + j // fan], t1[first + j], across, preferred_element_type=jnp.float32
+            ).astype(bf)
+            for j in range(2 * fan)
+        ]
+        fars = [
+            jnp.dot(moments[j], basis[first + j], preferred_element_type=jnp.float32)
+            for j in range(2 * fan)
+        ]
         for j in range(2 * fan):
-            t = w * 2 * fan + j
-            moment = lax.dot_general(
-                local[w * 2 + j // fan], t1[t], across, preferred_element_type=jnp.float32
-            ).astype(bf)
-            far = jnp.dot(moment, basis[t], preferred_element_type=jnp.float32)
-            out_ref[t] = jnp.where(point < counts[t], near[t] + far, 0.0)
+            t = first + j
+            out_ref[t] = jnp.where(point < counts[t], near[t] + fars[j], 0.0)
         return 0
 
     lax.fori_loop(0, boxes // 2, body, 0)
@@ -476,8 +504,6 @@
 
     blocks = gather_ring(charges, "sub")
     planes = jnp.transpose(coords, (1, 0, 2))
-    left_c = slide(planes, "leaf", 1)
-    right_c = slide(planes, "leaf", -1)
     own_counts = lax.dynamic_slice_in_dim(counts, start, leaf_dev, 0)
 
     slot = jnp.arange(group_size, dtype=jnp.int32)
@@ -486,10 +512,9 @@
     plan_own, plan_all = plan_near(near_list, (group - 1) * group_size, group_size, own_counts)
 
     blocks, plan_own, plan_all = tie((blocks, plan_own, plan_all))
-    mine = arrange(place, counts, blocks)
-    mine, left_c, right_c = tie((mine, left_c, right_c))
-    left_q = slide(mine, "leaf", 1)
-    right_q = slide(mine, "leaf", -1)
+    mine = arrange(place, counts, blocks, planes)
+    left = slide(mine, "leaf", 1)
+    right = slide(mine, "leaf", -1)
 
     own_charges = lax.dynamic_slice_in_dim(mine, start, leaf_dev, 0)
     transfer_boxed = transfer1.reshape(clusters, 8, rank_size, rank_size)
@@ -519,6 +544,10 @@
     ).astype(jnp.bfloat16)
 
     far2_local = jnp.clip(far2_list - (group - 1) * group_boxes, 0, 3 * group_boxes - 1)
+    odd = lax.rem(group, 2) == 1
+    block = far2_local // group_boxes
+    block = jnp.where(odd, 2 - block, block)
+    far2_local = block * group_boxes + far2_local % group_boxes
     picks = jnp.where(far2_list >= 0, far2_local, 3 * group_boxes).reshape(-1)
     table = top_moment[None]
     box_far = None
@@ -527,21 +556,27 @@
             table, acc, box_far = tie((table, acc, box_far))
         else:
             table, acc = tie((table, acc))
+        moves = (2, 3) if k == 0 else (1, 2, 3)
+        if k == 0:
+            both = jnp.concatenate([group_moments, table], axis=0)
+            partner = lax.ppermute(both, "leaf", [(i, i ^ 1) for i in range(leaves)])
+            pairs = [(i, i + 1 if i % 2 else i - 1) for i in range(1, leaves - 1)]
+            side = lax.ppermute(group_moments, "leaf", pairs)
         others = [
             lax.ppermute(table, "leaf", [(i, i ^ (m << 2 * k)) for i in range(leaves)])
-            for m in (1, 2, 3)
+            for m in moves
         ]
         if k == 0:
-            left_b = slide(group_moments, "leaf", 1)
-            right_b = slide(group_moments, "leaf", -1)
             acc, src_c, src_q = near_first(
-                share_of(k), plan_all, (left_c, planes, right_c), (left_q, mine, right_q), acc
+                share_of(k), plan_all, (left, mine, right), acc, group_size
             )
-            others, left_b, right_b, acc = tie((others, left_b, right_b, acc))
+            others, partner, side, acc = tie((others, partner, side, acc))
+            others = [partner[group_boxes:]] + list(others)
+            partner = partner[:group_boxes]
         else:
             acc = near_next(share_of(k), plan_all, src_c, src_q, acc)
         if k == 1:
-            box_far = box_field(picks, left_b, group_moments, right_b, coupling2)
+            box_far = box_field(picks, side, group_moments, partner, coupling2)
         table = jnp.concatenate([table] + list(others), axis=0)
     flips = jnp.where(far3_list[0] >= 0, far3_list[0] ^ group, -1)
     lane_box = (lane * clusters)[None]

time: 144 us -> 124 us (0.86)
  starting transfers between devices: 49.8 us -> 34.9 us
  Pallas kernels: 76.6 us -> 62.7 us
  other arithmetic: 7.43 us -> 13.3 us
  local copies, waits for them, and re-layouts: 5.56 us -> 8.06 us
    pallas_call x1, Pallas kernels: 19.5 us -> 4.73 us  [go_down(): pl.pallas_call(down_kernel, out_shape=jax.ShapeDtypeStruct((leaves,) + ne...]
    ppermute x6 -> x2, starting transfers between devices: 18.3 us -> 6.99 us  [slide(): return lax.ppermute(x, axis, pairs)]
    ppermute x9 -> x8, starting transfers between devices: 23.4 us -> 16.5 us  [on_device(): lax.ppermute(table, 'leaf', [(i, i ^ m << 2 * k) for i in range(leaves)])]
    ppermute x0 -> x2, starting transfers between devices: none -> 3.29 us  [the longest x1 2.53 us: on_device(): side = lax.ppermute(group_moments, 'leaf', pairs)]
    another operation x3, other arithmetic: 0.23 us -> 1.88 us  [share_of(): return jnp.stack([jnp.int32(k), jnp.int32(k + 1), jnp.int32(rounds), start])]
    pallas_call x2, Pallas kernels: 24.1 us -> 25.5 us  [near_next(): pl.pallas_call(near_next_kernel, out_shape=jax.ShapeDtypeStruct(acc.shape...]
    unnamed x23 -> x43, local copies, waits for them, and re-layouts: 4.13 us -> 4.78 us
  transfers between devices with their start and end apart: 21 -> 18, of which waited for: 0 -> 0; matrix products, arithmetic and copies ran while one was open for 9% -> 17% of each run, Pallas kernels for 40% -> 46%
where the time goes in v3:
time: 124 us; the launch traced here: 121 us
  Pallas kernels  62.7 us (51%)
  starting transfers between devices  34.9 us (28%)
  other arithmetic  13.3 us (11%)
  local copies, waits for them, and re-layouts  8.06 us (6%)
  matrix products  1.93 us (2%)
    pallas_call x2, Pallas kernels, near_next(): pl.pallas_call(near_next_kernel, out_shape=jax.ShapeDtypeStruct(acc.shape...  25.5 us
    pallas_call x1, Pallas kernels, near_own(): pl.pallas_call(near_own_kernel, out_shape=jax.ShapeDtypeStruct((targets +...  17.5 us
    ppermute x8, starting transfers between devices, on_device(): lax.ppermute(table, 'leaf', [(i, i ^ m << 2 * k) for i in range(leaves)])  16.5 us
    pallas_call x1, Pallas kernels, near_first(): pl.pallas_call(near_first_kernel, out_shape=(jax.ShapeDtypeStruct(acc.sha...  11.5 us
    ppermute x6, starting transfers between devices, shift(): return lax.ppermute(x, axis, [(i, (i + by) % count) for i in range(count)])  8.06 us
    ppermute x2, starting transfers between devices, slide(): return lax.ppermute(x, axis, pairs)  6.99 us
    unnamed x43, local copies, waits for them, and re-layouts  4.78 us
    pallas_call x1, Pallas kernels, go_down(): pl.pallas_call(down_kernel, out_shape=jax.ShapeDtypeStruct((leaves,) + ne...  4.73 us
  transfers between devices with their start and end apart: 18, of which 0 were waited for; matrix products, arithmetic and copies ran while one was open for 17% of the time, Pallas kernels for 46%

profile of v3, /device:TPU:1, one launch (start us, length us, event | category | flops | bytes accessed | tf_op | source)
XLA Modules:
  0.0 121.4 jit_solution(16252157786547929587)
XLA Ops:
  0.0 3.6 %collective-permute-start = (bf16[128,8,128]{2,1,0:T(8,128)(2,1)}, bf16[128,8,128]{2,1,0:T(8,128)(2,1)S(1)}, u32[]{:S(2)}, u32[]{:S(2)}) collective-permute-start(bf16[128,8,128]{2,1,0:T(8,128)(2,1)} %b0), channel_id=1, source_target_pairs={{0,3},{1,0},{2,1},{3,2},{4,7},{5,4},{6,5},{7,6},{8,11},{9,8},{10,9... | collective-permute-start | bytes 786440 | tf_op jit(solution)/shard_map/ppermute | solution.py:27
  6.1 1.3 %fusion.31 = (s32[128]{0:T(128)S(1)}, s32[128]{0:T(128)}) fusion(s32[512]{0:T(512)} %counts.1, s32[]{:T(128)S(6)} %select_n.135), kind=kLoop, calls=%fused_computation.116 | loop fusion | flops 640 | bytes 1540 | tf_op jit(solution)/shard_map/add | solution.py:454
  12.8 1.2 fusion.30.flips
  14.4 1.2 fusion.28.b
  15.6 1.3 %fusion.15 = s32[16,16]{1,0:T(8,128)} fusion(s32[16,16]{1,0:T(8,128)} %param.19, s32[]{:T(128)S(6)} %mul.44, pred[]{:T(512)S(6)} %eq.40), kind=kLoop, calls=%fused_computation.59 | loop fusion | flops 6912 | bytes 2053 | tf_op jit(solution)/shard_map/jit(_where)/select_n | solution.py:551
  16.9 1.3 %fusion.29.b = s32[5]{0:T(128)} fusion(s32[1]{0:T(128)} %constant.182.clone.1, s32[1]{0:T(128)} %slice.13, s32[3]{0:T(128)S(1)} %get-tuple-element.94), kind=kLoop, calls=%fused_computation.114 | loop fusion | flops 10 | bytes 40 | tf_op jit(solution)/shard_map/concatenate | solution.py:429
  19.5 3.9 %copy.26.t1 = bf16[128,64,64]{2,1,0:T(8,128)(2,1)S(1)} copy(bf16[128,64,64]{0,2,1:T(8,128)(2,1)} %param.18) | data formatting | bytes 2097152 | tf_op args[6]
  25.8 1.6 %arrange.1.q_ref.x1 = bf16[704,8,128]{2,1,0:T(8,128)(2,1)S(1)} custom-call(s32[512]{0:T(512)S(1)} %fusion.23.place, s32[512]{0:T(512)S(1)} %copy-done.7, bf16[128,8,128]{2,1,0:T(8,128)(2,1)S(1)} %copy-done.4, bf16[128,8,128]{2,1,0:T(8,128)(2,1)S(1)} %collective-permute-done.b1, bf16[128,8,128]{2,1,0:T(8,128)(2,1)S(1)} %collective-permute-done.1.b2, ...), custom_call_target="tpu_custom_call" | custom-call | flops 1048576 | bytes 2097152 | tf_op jit(solution)/shard_map/arrange/pallas_call | solution.py:92
  27.5 1.2 convolution_convert_fusion
  29.1 2.0 %collective-permute-start.3 = (bf16[16,8,64]{2,1,0:T(8,128)(2,1)S(1)}, bf16[16,8,64]{2,1,0:T(8,128)(2,1)S(1)}, u32[]{:S(2)}, u32[]{:S(2)}) collective-permute-start(bf16[16,8,64]{2,1,0:T(8,128)(2,1)S(1)} %fusion), channel_id=1, source_target_pairs={{0,3},{1,0},{2,1},{3,2},{4,7},{5,4},{6,5},{7,6},{8,11},{9,8},{10,9... | collective-permute-start | bytes 49160 | tf_op jit(solution)/shard_map/ppermute | solution.py:27
  31.2 1.4 %collective-permute-start.4 = (bf16[16,8,64]{2,1,0:T(8,128)(2,1)S(1)}, bf16[16,8,64]{2,1,0:T(8,128)(2,1)S(1)}, u32[]{:S(2)}, u32[]{:S(2)}) collective-permute-start(bf16[16,8,64]{2,1,0:T(8,128)(2,1)S(1)} %fusion), channel_id=1, source_target_pairs={{0,2},{1,3},{2,0},{3,1},{4,6},{5,7},{6,4},{7,5},{8,10},{9,11},{10,... | collective-permute-start | bytes 49160 | tf_op jit(solution)/shard_map/ppermute | solution.py:27
  32.6 5.1 %collective-permute-start.10 = (bf16[704,8,128]{2,1,0:T(8,128)(2,1)S(1)}, bf16[704,8,128]{2,1,0:T(8,128)(2,1)S(1)}, u32[]{:S(2)}, u32[]{:S(2)}) collective-permute-start(bf16[704,8,128]{2,1,0:T(8,128)(2,1)S(1)} %arrange.1.q_ref.x1), channel_id=1, source_target_pairs={{0,4},{4,8},{8,12},{12,16},{16,20},{20,24},{24,28},{28,32},{32,36}... | collective-permute-start | bytes 4325384 | tf_op jit(solution)/shard_map/ppermute | solution.py:33
  37.7 1.9 %collective-permute-start.11 = (bf16[704,8,128]{2,1,0:T(8,128)(2,1)S(1)}, bf16[704,8,128]{2,1,0:T(8,128)(2,1)S(1)}, u32[]{:S(2)}, u32[]{:S(2)}) collective-permute-start(bf16[704,8,128]{2,1,0:T(8,128)(2,1)S(1)} %arrange.1.q_ref.x1), channel_id=1, source_target_pairs={{4,0},{8,4},{12,8},{16,12},{20,16},{24,20},{28,24},{32,28},{36,32}... | collective-permute-start | bytes 4325384 | tf_op jit(solution)/shard_map/ppermute | solution.py:33
  39.6 17.5 %near_own.1.acc_in = f32[129,8,128]{2,1,0:T(8,128)S(1)} custom-call(s32[4]{0:T(128)S(1)} %copy-done.12, s32[912]{0:T(1024)S(1)} %get-tuple-element.46.w, s32[4128]{0:T(1024)S(1)} %compare_select_fusion.l, s32[5]{0:T(128)S(1)} %copy-done.15, s32[129]{0:T(256)S(1)} %copy-done.9, s32[128]{0:T(128)S(1)} %copy-done.16, bf16[3,512,128]{2,1,0:T(8,128)(2,1)S(1)} %bitcast.49, ...), custom_call_target="tpu_custom_call" | custom-call | flops 4294967296 | bytes 1048576 | tf_op jit(solution)/shard_map/near_own/pallas_call | solution.py:254
  57.4 2.5 %collective-permute-start.9 = (bf16[64,8,64]{2,1,0:T(8,128)(2,1)S(1)}, bf16[64,8,64]{2,1,0:T(8,128)(2,1)S(1)}, u32[]{:S(2)}, u32[]{:S(2)}) collective-permute-start(bf16[64,8,64]{2,1,0:T(8,128)(2,1)S(1)} %bitcast.44), channel_id=1, source_target_pairs={{4,8},{8,4},{12,16},{16,12},{20,24},{24,20},{28,32},{32,28},{36,40... | collective-permute-start | bytes 196616 | tf_op jit(solution)/shard_map/ppermute | solution.py:564
  60.2 2.2 %collective-permute-start.6 = (bf16[1,8,64]{2,1,0:T(8,128)(2,1)S(1)}, bf16[1,8,64]{2,1,0:T(8,128)(2,1)S(1)}, u32[]{:S(2)}, u32[]{:S(2)}) collective-permute-start(bf16[1,8,64]{2,1,0:T(8,128)(2,1)S(1)} %fusion.2), channel_id=1, source_target_pairs={{0,8},{4,12},{8,0},{12,4},{16,24},{20,28},{24,16},{28,20},{32,40},... | collective-permute-start | bytes 3080 | tf_op jit(solution)/shard_map/ppermute | solution.py:566
  63.3 11.5 %near_first.1 = (f32[129,8,128]{2,1,0:T(8,128)S(1)}, f32[3,1544,128]{2,1,0:T(8,128)S(1)}, bf16[1537,8,128]{2,1,0:T(8,128)(2,1)S(1)}) custom-call(s32[4]{0:T(128)S(1)} %copy-done.12, s32[912]{0:T(1024)S(1)} %get-tuple-element.58.w, s32[4128]{0:T(1024)S(1)} %copy-done.6, s32[5]{0:T(128)S(1)} %copy-done.14, s32[129]{0:T(256)S(1)} %copy-done.9, ...), custom_call_target="tpu_custom_call" | custom-call | flops 4294967296 | bytes 1048576 | tf_op jit(solution)/shard_map/near_first/pallas_call | solution.py:276
  74.8 6.4 %collective-permute-start.12 = (bf16[4,8,64]{2,1,0:T(8,128)(2,1)S(1)}, bf16[4,8,64]{2,1,0:T(8,128)(2,1)S(1)}, u32[]{:S(2)}, u32[]{:S(2)}) collective-permute-start(bf16[4,8,64]{2,1,0:T(8,128)(2,1)S(1)} %pad_maximum_fusion.3), channel_id=1, source_target_pairs={{0,16},{4,20},{8,24},{12,28},{16,0},{20,4},{24,8},{28,12},{32,48},... | collective-permute-start | bytes 12296 | tf_op jit(solution)/shard_map/ppermute | solution.py:566
  82.5 12.6 %near_next.2.acc_in = f32[129,8,128]{2,1,0:T(8,128)S(1)} custom-call(s32[4]{0:T(128)S(1)} %copy-done.11, s32[912]{0:T(1024)S(1)} %get-tuple-element.58.w, s32[4128]{0:T(1024)S(1)} %copy-done.6, s32[5]{0:T(128)S(1)} %copy-done.14, s32[129]{0:T(256)S(1)} %copy-done.9, s32[128]{0:T(128)S(1)} %copy-done.16, f32[3,1544,128]{2,1,0:T(8,128)S(1)} %get-tuple-element.70.src_c, ...), custom_call_target="tpu_custom_call" | custom-call | flops 4294967296 | bytes 1048576 | tf_op jit(solution)/shard_map/near_next/pallas_call | solution.py:301
  95.1 1.7 %box_field.1.box_far = f32[16,8,64]{2,1,0:T(8,128)S(1)} custom-call(s32[256]{0:T(256)S(1)} %reshape.100.picks, bf16[64,8,64]{2,1,0:T(8,128)(2,1)S(1)} %collective-permute-done.9.left, bf16[64,8,64]{2,1,0:T(8,128)(2,1)S(1)} %bitcast.47, bf16[64,8,64]{2,1,0:T(8,128)(2,1)S(1)} %slice.15.right, bf16[256,64,64]{2,1,0:T(8,128)(2,1)S(1)} %bitcast.43), custom_call_target="tpu_custom_call" | custom-call | flops 16777216 | bytes 4194304 | tf_op jit(solution)/shard_map/box_field/pallas_call | solution.py:349
  96.9 3.3 %collective-permute-start.15 = (bf16[16,8,64]{2,1,0:T(8,128)(2,1)S(1)}, bf16[16,8,64]{2,1,0:T(8,128)(2,1)S(1)}, u32[]{:S(2)}, u32[]{:S(2)}) collective-permute-start(bf16[16,8,64]{2,1,0:T(8,128)(2,1)S(1)} %pad_maximum_fusion.2), channel_id=1, source_target_pairs={{0,64},{4,68},{8,72},{12,76},{16,80},{20,84},{24,88},{28,92},{32,9... | collective-permute-start | bytes 49160 | tf_op jit(solution)/shard_map/ppermute | solution.py:566
  100.2 2.6 %collective-permute-start.16 = (bf16[16,8,64]{2,1,0:T(8,128)(2,1)S(1)}, bf16[16,8,64]{2,1,0:T(8,128)(2,1)S(1)}, u32[]{:S(2)}, u32[]{:S(2)}) collective-permute-start(bf16[16,8,64]{2,1,0:T(8,128)(2,1)S(1)} %pad_maximum_fusion.2), channel_id=1, source_target_pairs={{0,128},{4,132},{8,136},{12,140},{16,144},{20,148},{24,152},{28,15... | collective-permute-start | bytes 49160 | tf_op jit(solution)/shard_map/ppermute | solution.py:566
  103.6 13.0 %near_next.3.near = f32[129,8,128]{2,1,0:T(8,128)S(1)} custom-call(s32[4]{0:T(128)S(1)} %copy-done.13, s32[912]{0:T(1024)S(1)} %get-tuple-element.58.w, s32[4128]{0:T(1024)S(1)} %copy-done.6, s32[5]{0:T(128)S(1)} %copy-done.14, s32[129]{0:T(256)S(1)} %copy-done.9, s32[128]{0:T(128)S(1)} %copy-done.16, f32[3,1544,128]{2,1,0:T(8,128)S(1)} %get-tuple-element.70.src_c, ...), custom_call_target="tpu_custom_call" | custom-call | flops 4294967296 | bytes 1048576 | tf_op jit(solution)/shard_map/near_next/pallas_call | solution.py:301
  116.7 4.7 %go_down.1 = f32[128,8,128]{2,1,0:T(8,128)} custom-call(s32[8]{0:T(128)S(1)} %copy-done.10, s32[128]{0:T(128)S(1)} %copy-done.8, s32[1]{0:T(128)} %bitcast.1.share, bf16[64,8,64]{2,1,0:T(8,128)(2,1)S(1)} %pad_maximum_fusion.1.table, bf16[8,64,64]{2,1,0:T(8,128)(2,1)S(1)} %bitcast.50, bf16[64,64,64]{2,1,0:T(8,128)(2,1)S(1)} %copy-done.1, ...), custom_call_target="tpu_custom_call" | custom-call | flops 67108864 | bytes 5242880 | tf_op jit(solution)/shard_map/go_down/pallas_call | solution.py:405
  (107 shorter events, 15.8 us)
Async XLA Ops:
  0.0 25.1 %copy-start.4 = (bf16[128,8,128]{2,1,0:T(8,128)(2,1)S(1)}, bf16[128,8,128]{2,1,0:T(8,128)(2,1)}, u32[]{:S(2)}) copy-start(bf16[128,8,128]{2,1,0:T(8,128)(2,1)} %b0) | copy-start | bytes 786436
  0.0 25.1 %copy-start.3 = (bf16[512,3,128]{2,0,1:T(8,128)(2,1)S(1)}, bf16[512,3,128]{2,0,1:T(8,128)(2,1)}, u32[]{:S(2)}) copy-start(bf16[512,3,128]{2,0,1:T(8,128)(2,1)} %param.12) | copy-start | bytes 1179652
  0.0 25.1 %collective-permute-start = (bf16[128,8,128]{2,1,0:T(8,128)(2,1)}, bf16[128,8,128]{2,1,0:T(8,128)(2,1)S(1)}, u32[]{:S(2)}, u32[]{:S(2)}) collective-permute-start(bf16[128,8,128]{2,1,0:T(8,128)(2,1)} %b0), channel_id=1, source_target_pairs={{0,3},{1,0},{2,1},{3,2},{4,7},{5,4},{6,5},{7,6},{8,11},{9,8},{10,9... | collective-permute-start | bytes 786440 | tf_op jit(solution)/shard_map/ppermute | solution.py:27
  3.6 21.5 %collective-permute-start.1 = (bf16[128,8,128]{2,1,0:T(8,128)(2,1)}, bf16[128,8,128]{2,1,0:T(8,128)(2,1)S(1)}, u32[]{:S(2)}, u32[]{:S(2)}) collective-permute-start(bf16[128,8,128]{2,1,0:T(8,128)(2,1)} %b0), channel_id=1, source_target_pairs={{0,2},{1,3},{2,0},{3,1},{4,6},{5,7},{6,4},{7,5},{8,10},{9,11},{10,... | collective-permute-start | bytes 786440 | tf_op jit(solution)/shard_map/ppermute | solution.py:27
  3.9 21.2 %collective-permute-start.2 = (bf16[128,8,128]{2,1,0:T(8,128)(2,1)}, bf16[128,8,128]{2,1,0:T(8,128)(2,1)S(1)}, u32[]{:S(2)}, u32[]{:S(2)}) collective-permute-start(bf16[128,8,128]{2,1,0:T(8,128)(2,1)} %b0), channel_id=1, source_target_pairs={{0,1},{1,2},{2,3},{3,0},{4,5},{5,6},{6,7},{7,4},{8,9},{9,10},{10,1... | collective-permute-start | bytes 786440 | tf_op jit(solution)/shard_map/ppermute | solution.py:27
  29.1 28.1 %collective-permute-start.3 = (bf16[16,8,64]{2,1,0:T(8,128)(2,1)S(1)}, bf16[16,8,64]{2,1,0:T(8,128)(2,1)S(1)}, u32[]{:S(2)}, u32[]{:S(2)}) collective-permute-start(bf16[16,8,64]{2,1,0:T(8,128)(2,1)S(1)} %fusion), channel_id=1, source_target_pairs={{0,3},{1,0},{2,1},{3,2},{4,7},{5,4},{6,5},{7,6},{8,11},{9,8},{10,9... | collective-permute-start | bytes 49160 | tf_op jit(solution)/shard_map/ppermute | solution.py:27
  31.2 26.1 %collective-permute-start.4 = (bf16[16,8,64]{2,1,0:T(8,128)(2,1)S(1)}, bf16[16,8,64]{2,1,0:T(8,128)(2,1)S(1)}, u32[]{:S(2)}, u32[]{:S(2)}) collective-permute-start(bf16[16,8,64]{2,1,0:T(8,128)(2,1)S(1)} %fusion), channel_id=1, source_target_pairs={{0,2},{1,3},{2,0},{3,1},{4,6},{5,7},{6,4},{7,5},{8,10},{9,11},{10,... | collective-permute-start | bytes 49160 | tf_op jit(solution)/shard_map/ppermute | solution.py:27
  32.6 24.7 %collective-permute-start.5 = (bf16[16,8,64]{2,1,0:T(8,128)(2,1)S(1)}, bf16[16,8,64]{2,1,0:T(8,128)(2,1)S(1)}, u32[]{:S(2)}, u32[]{:S(2)}) collective-permute-start(bf16[16,8,64]{2,1,0:T(8,128)(2,1)S(1)} %fusion), channel_id=1, source_target_pairs={{0,1},{1,2},{2,3},{3,0},{4,5},{5,6},{6,7},{7,4},{8,9},{9,10},{10,1... | collective-permute-start | bytes 49160 | tf_op jit(solution)/shard_map/ppermute | solution.py:27
  32.6 29.9 %collective-permute-start.10 = (bf16[704,8,128]{2,1,0:T(8,128)(2,1)S(1)}, bf16[704,8,128]{2,1,0:T(8,128)(2,1)S(1)}, u32[]{:S(2)}, u32[]{:S(2)}) collective-permute-start(bf16[704,8,128]{2,1,0:T(8,128)(2,1)S(1)} %arrange.1.q_ref.x1), channel_id=1, source_target_pairs={{0,4},{4,8},{8,12},{12,16},{16,20},{20,24},{24,28},{28,32},{32,36}... | collective-permute-start | bytes 4325384 | tf_op jit(solution)/shard_map/ppermute | solution.py:33
  37.7 25.6 %collective-permute-start.11 = (bf16[704,8,128]{2,1,0:T(8,128)(2,1)S(1)}, bf16[704,8,128]{2,1,0:T(8,128)(2,1)S(1)}, u32[]{:S(2)}, u32[]{:S(2)}) collective-permute-start(bf16[704,8,128]{2,1,0:T(8,128)(2,1)S(1)} %arrange.1.q_ref.x1), channel_id=1, source_target_pairs={{4,0},{8,4},{12,8},{16,12},{20,16},{24,20},{28,24},{32,28},{36,32}... | collective-permute-start | bytes 4325384 | tf_op jit(solution)/shard_map/ppermute | solution.py:33
  39.6 20.3 %copy-start.1 = (bf16[64,64,64]{2,1,0:T(8,128)(2,1)S(1)}, bf16[64,64,64]{2,1,0:T(8,128)(2,1)}, u32[]{:S(2)}) copy-start(bf16[64,64,64]{2,1,0:T(8,128)(2,1)} %t2.1) | copy-start | bytes 1572868
  57.4 17.4 %collective-permute-start.9 = (bf16[64,8,64]{2,1,0:T(8,128)(2,1)S(1)}, bf16[64,8,64]{2,1,0:T(8,128)(2,1)S(1)}, u32[]{:S(2)}, u32[]{:S(2)}) collective-permute-start(bf16[64,8,64]{2,1,0:T(8,128)(2,1)S(1)} %bitcast.44), channel_id=1, source_target_pairs={{4,8},{8,4},{12,16},{16,12},{20,24},{24,20},{28,32},{32,28},{36,40... | collective-permute-start | bytes 196616 | tf_op jit(solution)/shard_map/ppermute | solution.py:564
  60.2 14.5 %collective-permute-start.6 = (bf16[1,8,64]{2,1,0:T(8,128)(2,1)S(1)}, bf16[1,8,64]{2,1,0:T(8,128)(2,1)S(1)}, u32[]{:S(2)}, u32[]{:S(2)}) collective-permute-start(bf16[1,8,64]{2,1,0:T(8,128)(2,1)S(1)} %fusion.2), channel_id=1, source_target_pairs={{0,8},{4,12},{8,0},{12,4},{16,24},{20,28},{24,16},{28,20},{32,40},... | collective-permute-start | bytes 3080 | tf_op jit(solution)/shard_map/ppermute | solution.py:566
  62.4 12.3 %collective-permute-start.7 = (bf16[1,8,64]{2,1,0:T(8,128)(2,1)S(1)}, bf16[1,8,64]{2,1,0:T(8,128)(2,1)S(1)}, u32[]{:S(2)}, u32[]{:S(2)}) collective-permute-start(bf16[1,8,64]{2,1,0:T(8,128)(2,1)S(1)} %fusion.2), channel_id=1, source_target_pairs={{0,12},{4,8},{8,4},{12,0},{16,28},{20,24},{24,20},{28,16},{32,44},... | collective-permute-start | bytes 3080 | tf_op jit(solution)/shard_map/ppermute | solution.py:566
  62.5 20.0 %copy-start.11 = (s32[4]{0:T(128)S(1)}, s32[4]{0:T(128)}, u32[]{:S(2)}) copy-start(s32[4]{0:T(128)} %fusion.27.share) | copy-start | bytes 52
  62.5 12.3 %collective-permute-start.8 = (bf16[65,8,64]{2,1,0:T(8,128)(2,1)S(1)}, bf16[65,8,64]{2,1,0:T(8,128)(2,1)S(1)}, u32[]{:S(2)}, u32[]{:S(2)}) collective-permute-start(bf16[65,8,64]{2,1,0:T(8,128)(2,1)S(1)} %pad_maximum_fusion), channel_id=1, source_target_pairs={{0,4},{4,0},{8,12},{12,8},{16,20},{20,16},{24,28},{28,24},{32,36},... | collective-permute-start | bytes 199688 | tf_op jit(solution)/shard_map/ppermute | solution.py:562
  74.8 22.0 %collective-permute-start.12 = (bf16[4,8,64]{2,1,0:T(8,128)(2,1)S(1)}, bf16[4,8,64]{2,1,0:T(8,128)(2,1)S(1)}, u32[]{:S(2)}, u32[]{:S(2)}) collective-permute-start(bf16[4,8,64]{2,1,0:T(8,128)(2,1)S(1)} %pad_maximum_fusion.3), channel_id=1, source_target_pairs={{0,16},{4,20},{8,24},{12,28},{16,0},{20,4},{24,8},{28,12},{32,48},... | collective-permute-start | bytes 12296 | tf_op jit(solution)/shard_map/ppermute | solution.py:566
  81.2 15.6 %collective-permute-start.13 = (bf16[4,8,64]{2,1,0:T(8,128)(2,1)S(1)}, bf16[4,8,64]{2,1,0:T(8,128)(2,1)S(1)}, u32[]{:S(2)}, u32[]{:S(2)}) collective-permute-start(bf16[4,8,64]{2,1,0:T(8,128)(2,1)S(1)} %pad_maximum_fusion.3), channel_id=1, source_target_pairs={{0,32},{4,36},{8,40},{12,44},{16,48},{20,52},{24,56},{28,60},{32,0... | collective-permute-start | bytes 12296 | tf_op jit(solution)/shard_map/ppermute | solution.py:566
  81.8 15.1 %collective-permute-start.14 = (bf16[4,8,64]{2,1,0:T(8,128)(2,1)S(1)}, bf16[4,8,64]{2,1,0:T(8,128)(2,1)S(1)}, u32[]{:S(2)}, u32[]{:S(2)}) collective-permute-start(bf16[4,8,64]{2,1,0:T(8,128)(2,1)S(1)} %pad_maximum_fusion.3), channel_id=1, source_target_pairs={{0,48},{4,52},{8,56},{12,60},{16,32},{20,36},{24,40},{28,44},{32,1... | collective-permute-start | bytes 12296 | tf_op jit(solution)/shard_map/ppermute | solution.py:566
  96.9 19.8 %copy-start.5 = (bf16[1,8,64,64]{3,2,1,0:T(8,128)(2,1)S(1)}, bf16[1,8,64,64]{3,2,1,0:T(8,128)(2,1)}, u32[]{:S(2)}) copy-start(bf16[1,8,64,64]{3,2,1,0:T(8,128)(2,1)} %param.23) | copy-start | bytes 196612
  96.9 19.8 %copy-start.8 = (s32[128]{0:T(128)S(1)}, s32[128]{0:T(128)}, u32[]{:S(2)}) copy-start(s32[128]{0:T(128)} %get-tuple-element.89.counts) | copy-start | bytes 1540
  96.9 19.7 %collective-permute-start.15 = (bf16[16,8,64]{2,1,0:T(8,128)(2,1)S(1)}, bf16[16,8,64]{2,1,0:T(8,128)(2,1)S(1)}, u32[]{:S(2)}, u32[]{:S(2)}) collective-permute-start(bf16[16,8,64]{2,1,0:T(8,128)(2,1)S(1)} %pad_maximum_fusion.2), channel_id=1, source_target_pairs={{0,64},{4,68},{8,72},{12,76},{16,80},{20,84},{24,88},{28,92},{32,9... | collective-permute-start | bytes 49160 | tf_op jit(solution)/shard_map/ppermute | solution.py:566
  100.2 16.4 %collective-permute-start.16 = (bf16[16,8,64]{2,1,0:T(8,128)(2,1)S(1)}, bf16[16,8,64]{2,1,0:T(8,128)(2,1)S(1)}, u32[]{:S(2)}, u32[]{:S(2)}) collective-permute-start(bf16[16,8,64]{2,1,0:T(8,128)(2,1)S(1)} %pad_maximum_fusion.2), channel_id=1, source_target_pairs={{0,128},{4,132},{8,136},{12,140},{16,144},{20,148},{24,152},{28,15... | collective-permute-start | bytes 49160 | tf_op jit(solution)/shard_map/ppermute | solution.py:566
  102.8 13.8 %collective-permute-start.17 = (bf16[16,8,64]{2,1,0:T(8,128)(2,1)S(1)}, bf16[16,8,64]{2,1,0:T(8,128)(2,1)S(1)}, u32[]{:S(2)}, u32[]{:S(2)}) collective-permute-start(bf16[16,8,64]{2,1,0:T(8,128)(2,1)S(1)} %pad_maximum_fusion.2), channel_id=1, source_target_pairs={{0,192},{4,196},{8,200},{12,204},{16,208},{20,212},{24,216},{28,22... | collective-permute-start | bytes 49160 | tf_op jit(solution)/shard_map/ppermute | solution.py:566
  (11 other events, 105.4 us)
